TPU v7x, 256 devices: a whole 4x4x8 slice. The times are simulated.
256 devices in a mesh: lon: 32 (over y, x, core), lat: 8 (over z).
Axes of the slice: x: 4, y: 4, z: 8, core: 2. Of those that a mesh axis runs over, the one named last changes fastest.
Arguments:
- tracer: float32 [4096, 8192], P('lon', 'lat'), parts along dimension 1, may hold values from -7 to 7
- lower2: float32 [4096, 8192], P('lon', 'lat'), parts along dimension 1, may hold values from -4096 to -256
- lower1: float32 [4096, 8192], P('lon', 'lat'), parts along dimension 1, may hold values from -6144 to -256
- upper1: float32 [4096, 8192], P('lon', 'lat'), parts along dimension 1, may hold values from -4096 to -128
- upper2: float32 [4096, 8192], P('lon', 'lat'), parts along dimension 1, may hold values from -2048 to -64
Outputs:
- advanced: float32 [4096, 8192], P('lon', 'lat'), parts along dimension 1
There are 8 independent parts, one for each index of `lat`. A program takes and returns all parts, laid end to end along the dimension named above; each array names one. Nothing has to cross between parts.
All inputs are finite; a program needn't handle non-finite values.
Results may differ from a plain program's by a relative error of at most 0.0003.
Values sent between devices are 32-bit elements; how exact they have to be, the bound alone decides.
No kernel may reach another device: no remote copies, remote signals or barrier semaphores. Data moves between devices by JAX's collectives and lax.ppermute only.
A program may use at most 128 MiB of HBM per device.

v0:
```python
import math

import jax
import jax.numpy as jnp
from jax import lax
from jax.sharding import PartitionSpec as P


def passed_along(array, axis, by):
    peers = lax.axis_size(axis)
    pairs = [(i, i + by) for i in range(peers) if 0 <= i + by < peers]
    return lax.ppermute(array, axis, pairs)


def padded_2(cells, sides, width):
    for axis, dim in sides:
        count = lax.axis_size(axis)
        ends = count - 1
        head = lax.slice_in_dim(cells, 0, width, axis=dim)
        tail = lax.slice_in_dim(cells, cells.shape[dim] - width, cells.shape[dim], axis=dim)
        cells = jnp.concatenate(
            [
                lax.ppermute(tail, axis, [(i, (i + 1) % count) for i in range(ends)]),
                cells,
                lax.ppermute(head, axis, [((i + 1) % count, i) for i in range(ends)]),
            ],
            axis=dim,
        )
    return cells


def matmul_small(left, right):
    total = None
    for inner_idx in range(left.shape[-2]):
        term = left[..., inner_idx : inner_idx + 1, :] * right[..., inner_idx : inner_idx + 1, :, :]
        total = term if total is None else total + term
    return total


def solve_small(matrix, rhs_cols):
    rows_left = [matrix[..., row_pos, :, :] for row_pos in range(4)]
    rows_right = [rhs_cols[..., row_pos, :, :] for row_pos in range(4)]
    for pivot_col in range(4):
        pivot_value = rows_left[pivot_col][..., pivot_col : pivot_col + 1, :]
        rows_left[pivot_col] = rows_left[pivot_col] / pivot_value
        rows_right[pivot_col] = rows_right[pivot_col] / pivot_value
        for other_row in range(4):
            if other_row != pivot_col:
                factor = rows_left[other_row][..., pivot_col : pivot_col + 1, :]
                rows_left[other_row] = rows_left[other_row] - factor * rows_left[pivot_col]
                rows_right[other_row] = rows_right[other_row] - factor * rows_right[pivot_col]
    return jnp.stack(rows_right, axis=-3)


def start_blocks(reduced):
    line_count = reduced.shape[-1]
    empty_pair = jnp.zeros(reduced.shape[:-2] + (2, line_count), jnp.float32)
    upper_block = jnp.concatenate([reduced[..., 1:3, :], empty_pair], axis=-2)
    lower_block = jnp.concatenate([empty_pair, reduced[..., 3:5, :]], axis=-2)
    target = reduced[..., 0:1, :]
    diag_block = jnp.broadcast_to(jnp.eye(4, dtype=jnp.float32)[:, :, None], upper_block.shape)
    return (diag_block, upper_block, lower_block, target)


def scaled_rows(blocks):
    diag_block, upper_block, lower_block, target = blocks
    return solve_small(diag_block, jnp.concatenate([upper_block, lower_block, target], axis=-2))


def reduce_level(blocks, from_high, from_low):
    diag_block, upper_block, lower_block, target = blocks
    high_upper = from_high[..., 0:4, :]
    high_lower = from_high[..., 4:8, :]
    high_target = from_high[..., 8:9, :]
    low_upper = from_low[..., 0:4, :]
    low_lower = from_low[..., 4:8, :]
    low_target = from_low[..., 8:9, :]
    new_diag = (
        diag_block - matmul_small(upper_block, high_lower) - matmul_small(lower_block, low_upper)
    )
    new_upper = -matmul_small(upper_block, high_upper)
    new_lower = -matmul_small(lower_block, low_lower)
    new_target = (
        target - matmul_small(upper_block, high_target) - matmul_small(lower_block, low_target)
    )
    return (new_diag, new_upper, new_lower, new_target)


def run_blocks(step_fn, start_state, inputs):
    first = jax.tree.map(lambda array: array[0], inputs)
    final_state, outputs = step_fn(start_state, first)
    return (final_state, jax.tree.map(lambda array: array[None], outputs))


def sweep(coefs, rhs_list):
    row_count, line_count = rhs_list[0].shape
    inner_count = math.gcd(row_count, 128)
    outer_count = row_count // inner_count
    rhs_total = len(rhs_list)

    def to_blocks(array):
        return array.reshape(outer_count, inner_count, line_count)

    zero_vec = jnp.zeros((line_count,), jnp.float32)

    def forward(state, block_data):
        last_p, last_q, last_g, older_p, older_q, older_g = state
        far_low, near_low, centre, near_high, far_high = block_data[0:5]
        targets = block_data[5]
        list_p, list_q = ([], [])
        list_g = [[] for _ in range(rhs_total)]
        for step_idx in range(inner_count):
            beta_term = near_low[step_idx] - far_low[step_idx] * older_p
            pivot_value = centre[step_idx] - far_low[step_idx] * older_q - beta_term * last_p
            new_p = (near_high[step_idx] - beta_term * last_q) / pivot_value
            new_q = far_high[step_idx] / pivot_value
            new_g = tuple(
                (
                    (
                        targets[col_idx][step_idx]
                        - far_low[step_idx] * older_g[col_idx]
                        - beta_term * last_g[col_idx]
                    )
                    / pivot_value
                    for col_idx in range(rhs_total)
                )
            )
            older_p, older_q, older_g = (last_p, last_q, last_g)
            last_p, last_q, last_g = (new_p, new_q, new_g)
            list_p.append(new_p)
            list_q.append(new_q)
            for col_idx in range(rhs_total):
                list_g[col_idx].append(new_g[col_idx])
        new_state = (last_p, last_q, last_g, older_p, older_q, older_g)
        return (
            new_state,
            (jnp.stack(list_p), jnp.stack(list_q), tuple((jnp.stack(items) for items in list_g))),
        )

    zero_cols = tuple((zero_vec for _ in range(rhs_total)))
    start_state = (zero_vec, zero_vec, zero_cols, zero_vec, zero_vec, zero_cols)
    inputs = tuple((to_blocks(array) for array in coefs)) + (
        tuple((to_blocks(array) for array in rhs_list)),
    )
    _, (coef_p, coef_q, coef_g) = run_blocks(forward, start_state, inputs)

    def backward(state, block_data):
        after_one, after_two = state
        factor_p, factor_q, factor_g = block_data
        solved = [[None] * inner_count for _ in range(rhs_total)]
        for step_idx in reversed(range(inner_count)):
            current = tuple(
                (
                    factor_g[col_idx][step_idx]
                    - factor_p[step_idx] * after_one[col_idx]
                    - factor_q[step_idx] * after_two[col_idx]
                    for col_idx in range(rhs_total)
                )
            )
            for col_idx in range(rhs_total):
                solved[col_idx][step_idx] = current[col_idx]
            after_two = after_one
            after_one = current
        return ((after_one, after_two), tuple((jnp.stack(items) for items in solved)))

    _, solution = run_blocks(backward, (zero_cols, zero_cols), (coef_p, coef_q, coef_g))
    return tuple((array.reshape(row_count, line_count) for array in solution))


def neighbours(values, stride):
    from_high = passed_along(values, "lon", -stride)
    from_low = passed_along(values, "lon", stride)
    return (from_high, from_low)


def per_device(tracer, lower2, lower1, upper1, upper2):
    diagonal = 1.0 + (jnp.abs(lower2) + jnp.abs(lower1) + jnp.abs(upper1) + jnp.abs(upper2))
    row_count, line_count = tracer.shape
    padded = padded_2(tracer, (("lon", 0),), 2)
    applied = (
        lower2 * padded[0:-4]
        + lower1 * padded[1:-3]
        + diagonal * tracer
        + upper1 * padded[3:-1]
        + upper2 * padded[4:]
    )
    source = 2.0 * tracer - applied
    zeros_top = jnp.zeros((row_count - 2, line_count), jnp.float32)
    zeros_top_one = jnp.zeros((row_count - 1, line_count), jnp.float32)
    zeros_low = jnp.zeros((row_count - 2, line_count), jnp.float32)
    zeros_low_one = jnp.zeros((row_count - 1, line_count), jnp.float32)
    spike_east_one = jnp.concatenate(
        [zeros_top, upper2[row_count - 2 : row_count - 1], upper1[row_count - 1 :]], axis=0
    )
    spike_east_two = jnp.concatenate([zeros_top_one, upper2[row_count - 1 :]], axis=0)
    spike_west_two = jnp.concatenate([lower2[0:1], zeros_low_one], axis=0)
    spike_west_one = jnp.concatenate([lower1[0:1], lower2[1:2], zeros_low], axis=0)
    solution = sweep(
        (lower2, lower1, diagonal, upper1, upper2),
        (source, spike_east_one, spike_east_two, spike_west_two, spike_west_one),
    )
    reduced = jnp.stack(
        [jnp.concatenate([column[0:2], column[row_count - 2 :]], axis=0) for column in solution],
        axis=1,
    )
    blocks = start_blocks(reduced)
    for level_idx in range((lax.axis_size("lon") - 1).bit_length()):
        from_high, from_low = neighbours(scaled_rows(blocks), 1 << level_idx)
        blocks = reduce_level(blocks, from_high, from_low)
    interface = solve_small(blocks[0], blocks[3])
    from_high, from_low = neighbours(interface, 1)
    above = from_high[0:2, 0]
    below = from_low[2:4, 0]
    advanced = (
        solution[0]
        - solution[1] * above[0]
        - solution[2] * above[1]
        - solution[3] * below[0]
        - solution[4] * below[1]
    )
    return advanced


def solution(mesh):
    in_specs = (P("lon", "lat"), P("lon", "lat"), P("lon", "lat"), P("lon", "lat"), P("lon", "lat"))
    out_specs = P("lon", "lat")
    return jax.shard_map(
        per_device, mesh=mesh, in_specs=in_specs, out_specs=out_specs, check_vma=False
    )
```

profile of v0, /device:TPU:1, one launch (start us, length us, event | category | flops | bytes accessed | tf_op | source)
XLA Modules:
  0.0 151.8 jit_solution(2208706951830027036)
XLA Ops:
  0.0 0.8 fusion.141
  0.8 5.1 %collective-permute-start.1 = (f32[2,1024]{1,0:T(2,128)S(1)}, f32[2,1024]{1,0:T(2,128)S(1)}, u32[]{:S(2)}, u32[]{:S(2)}) collective-permute-start(f32[2,1024]{1,0:T(2,128)S(1)} %get-tuple-element.1839), channel_id=1, source_target_pairs={{8,0},{16,8},{24,16},{32,24},{40,32},{48,40},{56,48},{64,56},{72,6... | collective-permute-start | bytes 24584 | tf_op jit(solution)/shard_map/ppermute | solution.py:25
  6.0 1.9 %collective-permute-start = (f32[2,1024]{1,0:T(2,128)S(1)}, f32[2,1024]{1,0:T(2,128)S(1)}, u32[]{:S(2)}, u32[]{:S(2)}) collective-permute-start(f32[2,1024]{1,0:T(2,128)S(1)} %get-tuple-element.1840), channel_id=1, source_target_pairs={{0,8},{8,16},{16,24},{24,32},{32,40},{40,48},{48,56},{56,64},{64,7... | collective-permute-start | bytes 24584 | tf_op jit(solution)/shard_map/ppermute | solution.py:23
  7.9 1.2 fusion.159
  9.2 1.4 fusion.154
  10.6 1.4 fusion.166
  11.9 1.4 fusion.179
  14.0 0.6 copy-done.4
  15.0 0.6 copy-done.3
  16.1 0.6 copy-done
  16.7 0.6 fusion.210
  17.3 1.3 fusion.95
  18.6 0.6 slice.5112
  19.7 1.3 fusion.96
  21.0 0.7 slice.5118
  21.7 0.6 slice.5126
  22.3 1.3 bitcast_subtract_fusion.6
  23.6 0.6 slice.5142
  24.2 0.6 slice.5120
  24.8 1.2 multiply_subtract_fusion.931
  26.0 0.6 slice.5128
  26.6 0.6 slice.5138
  27.2 1.2 multiply_subtract_fusion.932
  28.4 1.2 multiply_subtract_fusion.929
  29.6 0.6 fusion.94
  30.2 0.6 slice.5146
  30.8 0.6 slice.5130
  31.4 0.6 slice.5140
  31.9 0.6 slice.5144
  34.0 0.6 subtract_divide_fusion.335
  35.5 0.7 multiply_subtract_fusion.679
  38.7 1.7 %multiply_subtract_fusion.299 = (f32[1024]{0:T(1024)S(1)}, f32[1024]{0:T(1024)S(1)}, f32[1024]{0:T(1024)}, f32[1024]{0:T(1024)}, f32[1024]{0:T(1024)}, /*index=5...) fusion(f32[1024]{0:T(1024)S(1)} %get-tuple-element.866, ...), kind=kLoop, calls=%fused_computation.881 | loop fusion | flops 344064 | bytes 1384448 | tf_op jit(solution)/shard_map/sub | solution.py:154
  40.5 1.7 %multiply_subtract_fusion.425 = (f32[1024]{0:T(1024)S(1)}, f32[1024]{0:T(1024)S(1)}, f32[1024]{0:T(1024)}, f32[1024]{0:T(1024)}, f32[1024]{0:T(1024)}, /*index=5...) fusion(f32[1024]{0:T(1024)S(1)} %get-tuple-element.866, ...), kind=kLoop, calls=%fused_computation.1010 | loop fusion | flops 344064 | bytes 1384448 | tf_op jit(solution)/shard_map/sub | solution.py:154
  44.3 1.9 %multiply_subtract_fusion.173 = (f32[1024]{0:T(1024)S(1)}, f32[1024]{0:T(1024)S(1)}, f32[1024]{0:T(1024)}, f32[1024]{0:T(1024)}, f32[1024]{0:T(1024)}, /*index=5...) fusion(f32[1024]{0:T(1024)S(1)} %get-tuple-element.866, ...), kind=kLoop, calls=%fused_computation.627 | loop fusion | flops 344064 | bytes 1384448 | tf_op jit(solution)/shard_map/sub | solution.py:154
  46.5 8.0 %multiply_subtract_fusion.3 = (f32[1,9,1024]{2,1,0:T(8,128)S(1)}, f32[1,9,1024]{2,1,0:T(8,128)S(1)}, f32[1,9,1024]{2,1,0:T(8,128)S(1)}, f32[1,9,1024]{2,1,0:T(8,128)S(1)}) fusion(f32[]{:T(128)} %bitcast.1056, f32[]{:T(128)} %bitcast.1051, f32[]{:T(128)} %bitcast.1046, f32[]{:T(128)} %bitcast.1045, f32[4,9,1024]{2,1,0:T(8,128)S(1)} %concatenate.141, ...), kind=kLoop, calls=%fused_computation.49 | loop fusion | flops 202752 | bytes 294964 | tf_op jit(solution)/shard_map/sub | solution.py:51
  54.5 1.8 %multiply_subtract_fusion.2 = (f32[1,9,1024]{2,1,0:T(8,128)S(1)}, f32[1,9,1024]{2,1,0:T(8,128)S(1)}) fusion(f32[1,9,1024]{2,1,0:T(8,128)S(1)} %get-tuple-element.46, f32[1,9,1024]{2,1,0:T(8,128)S(1)} %get-tuple-element.48, f32[1,9,1024]{2,1,0:T(8,128)S(1)} %get-tuple-element.47, f32[]{:T(128)} %bitcast.1063, f32[]{:T(128)} %bitcast.1062, f32[]{:T(128)} %bitcast.1064), kind=kLoop, calls=%fused_computation.48 | loop fusion | flops 55296 | bytes 184332 | tf_op jit(solution)/shard_map/sub | solution.py:51
  56.4 1.9 %collective-permute-start.3 = (f32[4,9,1024]{2,1,0:T(8,128)S(1)}, f32[4,9,1024]{2,1,0:T(8,128)S(1)}, u32[]{:S(2)}, u32[]{:S(2)}) collective-permute-start(f32[4,9,1024]{2,1,0:T(8,128)S(1)} %pad_maximum_fusion.1), channel_id=1, source_target_pairs={{0,8},{8,16},{16,24},{24,32},{32,40},{40,48},{48,56},{56,64},{64,7... | collective-permute-start | bytes 442376 | tf_op jit(solution)/shard_map/ppermute | solution.py:12
  58.3 2.4 %collective-permute-start.2 = (f32[4,9,1024]{2,1,0:T(8,128)S(1)}, f32[4,9,1024]{2,1,0:T(8,128)S(1)}, u32[]{:S(2)}, u32[]{:S(2)}) collective-permute-start(f32[4,9,1024]{2,1,0:T(8,128)S(1)} %pad_maximum_fusion.1), channel_id=1, source_target_pairs={{8,0},{16,8},{24,16},{32,24},{40,32},{48,40},{56,48},{64,56},{72,6... | collective-permute-start | bytes 442376 | tf_op jit(solution)/shard_map/ppermute | solution.py:12
  60.7 1.0 stack.2159
  62.8 5.2 %stack.2288 = f32[128,1024]{1,0:T(8,128)S(1)} concatenate(f32[1,1024]{1,0:T(1,128)S(1)} %bitcast.2737, f32[1,1024]{1,0:T(1,128)S(1)} %bitcast.2740, f32[1,1024]{1,0:T(1,128)S(1)} %bitcast.3414, f32[1,1024]{1,0:T(1,128)S(1)} %bitcast.3415, f32[1,1024]{1,0:T(1,128)S(1)} %bitcast.3416, f32[1,1024]{1,0:T(1,128)S(1)} %bitcast.3417, f32[1,1024]{1,0:T(1,128)S(1)} %bitcast.3418, ...), dimensions={0} | concatenate | bytes 1048576 | tf_op jit(solution)/shard_map/stack | solution.py:164
  69.1 5.2 %stack.2450 = f32[128,1024]{1,0:T(8,128)S(1)} concatenate(f32[1,1024]{1,0:T(1,128)S(1)} %bitcast.2731, f32[1,1024]{1,0:T(1,128)S(1)} %bitcast.2734, f32[1,1024]{1,0:T(1,128)S(1)} %bitcast.3210, f32[1,1024]{1,0:T(1,128)S(1)} %bitcast.3211, f32[1,1024]{1,0:T(1,128)S(1)} %bitcast.3212, f32[1,1024]{1,0:T(1,128)S(1)} %bitcast.3213, f32[1,1024]{1,0:T(1,128)S(1)} %bitcast.3214, ...), dimensions={0} | concatenate | bytes 1048576 | tf_op jit(solution)/shard_map/stack | solution.py:164
  74.4 0.7 copy-done.123
  76.3 2.5 %collective-permute-start.5 = (f32[4,9,1024]{2,0,1:T(4,128)S(1)}, f32[4,9,1024]{2,0,1:T(4,128)S(1)}, u32[]{:S(2)}, u32[]{:S(2)}) collective-permute-start(f32[4,9,1024]{2,0,1:T(4,128)S(1)} %pad_maximum_fusion.3), channel_id=1, source_target_pairs={{0,16},{8,24},{16,32},{24,40},{32,48},{40,56},{48,64},{56,72},{64,... | collective-permute-start | bytes 442376 | tf_op jit(solution)/shard_map/ppermute | solution.py:12
  78.8 1.3 collective-permute-start.4
  80.1 1.0 collective-permute-done.5
  81.3 3.4 %collective-permute-done.4 = f32[4,9,1024]{2,0,1:T(4,128)S(1)} collective-permute-done((f32[4,9,1024]{2,0,1:T(4,128)S(1)}, f32[4,9,1024]{2,0,1:T(4,128)S(1)}, u32[]{:S(2)}, u32[]{:S(2)}) %collective-permute-start.4) | collective-permute-done | bytes 147488 | tf_op jit(solution)/shard_map/ppermute | solution.py:12
  86.1 6.4 %collective-permute-start.7 = (f32[4,9,1024]{2,0,1:T(4,128)S(1)}, f32[4,9,1024]{2,0,1:T(4,128)S(1)}, u32[]{:S(2)}, u32[]{:S(2)}) collective-permute-start(f32[4,9,1024]{2,0,1:T(4,128)S(1)} %pad_maximum_fusion.5), channel_id=1, source_target_pairs={{0,32},{8,40},{16,48},{24,56},{32,64},{40,72},{48,80},{56,88},{64,... | collective-permute-start | bytes 442376 | tf_op jit(solution)/shard_map/ppermute | solution.py:12
  92.6 1.3 collective-permute-start.6
  93.9 0.8 collective-permute-done.7
  94.8 5.8 %collective-permute-done.6 = f32[4,9,1024]{2,0,1:T(4,128)S(1)} collective-permute-done((f32[4,9,1024]{2,0,1:T(4,128)S(1)}, f32[4,9,1024]{2,0,1:T(4,128)S(1)}, u32[]{:S(2)}, u32[]{:S(2)}) %collective-permute-start.6) | collective-permute-done | bytes 147488 | tf_op jit(solution)/shard_map/ppermute | solution.py:12
  102.2 3.5 %collective-permute-start.9 = (f32[4,9,1024]{2,0,1:T(4,128)S(1)}, f32[4,9,1024]{2,0,1:T(4,128)S(1)}, u32[]{:S(2)}, u32[]{:S(2)}) collective-permute-start(f32[4,9,1024]{2,0,1:T(4,128)S(1)} %pad_maximum_fusion.7), channel_id=1, source_target_pairs={{0,64},{8,72},{16,80},{24,88},{32,96},{40,104},{48,112},{56,120},{... | collective-permute-start | bytes 442376 | tf_op jit(solution)/shard_map/ppermute | solution.py:12
  105.7 1.3 collective-permute-start.8
  107.0 0.8 collective-permute-done.9
  107.9 3.7 %collective-permute-done.8 = f32[4,9,1024]{2,0,1:T(4,128)S(1)} collective-permute-done((f32[4,9,1024]{2,0,1:T(4,128)S(1)}, f32[4,9,1024]{2,0,1:T(4,128)S(1)}, u32[]{:S(2)}, u32[]{:S(2)}) %collective-permute-start.8) | collective-permute-done | bytes 147488 | tf_op jit(solution)/shard_map/ppermute | solution.py:12
  113.3 2.9 %collective-permute-start.11 = (f32[4,9,1024]{2,0,1:T(4,128)S(1)}, f32[4,9,1024]{2,0,1:T(4,128)S(1)}, u32[]{:S(2)}, u32[]{:S(2)}) collective-permute-start(f32[4,9,1024]{2,0,1:T(4,128)S(1)} %pad_maximum_fusion.9), channel_id=1, source_target_pairs={{0,128},{8,136},{16,144},{24,152},{32,160},{40,168},{48,176},{56,1... | collective-permute-start | bytes 442376 | tf_op jit(solution)/shard_map/ppermute | solution.py:12
  116.3 1.5 collective-permute-start.10
  118.4 5.2 %collective-permute-done.10 = f32[4,9,1024]{2,0,1:T(4,128)S(1)} collective-permute-done((f32[4,9,1024]{2,0,1:T(4,128)S(1)}, f32[4,9,1024]{2,0,1:T(4,128)S(1)}, u32[]{:S(2)}, u32[]{:S(2)}) %collective-permute-start.10) | collective-permute-done | bytes 147488 | tf_op jit(solution)/shard_map/ppermute | solution.py:12
  123.8 0.6 add_subtract_fusion
  124.9 13.5 %collective-permute-start.13 = (f32[4,1,1024]{2,1,0:T(1,128)S(1)}, f32[4,1,1024]{2,1,0:T(1,128)S(1)}, u32[]{:S(2)}, u32[]{:S(2)}) collective-permute-start(f32[4,1,1024]{2,1,0:T(1,128)S(1)} %pad_maximum_fusion.14), channel_id=1, source_target_pairs={{0,8},{8,16},{16,24},{24,32},{32,40},{40,48},{48,56},{56,64},{64,7... | collective-permute-start | bytes 49160 | tf_op jit(solution)/shard_map/ppermute | solution.py:12
  138.4 1.0 stack.2700
  140.4 5.3 %stack.2575 = f32[128,1024]{1,0:T(8,128)S(1)} concatenate(f32[1,1024]{1,0:T(1,128)S(1)} %bitcast.2725, f32[1,1024]{1,0:T(1,128)S(1)} %bitcast.2728, f32[1,1024]{1,0:T(1,128)S(1)} %bitcast.3128, f32[1,1024]{1,0:T(1,128)S(1)} %bitcast.3129, f32[1,1024]{1,0:T(1,128)S(1)} %bitcast.3130, f32[1,1024]{1,0:T(1,128)S(1)} %bitcast.3131, f32[1,1024]{1,0:T(1,128)S(1)} %bitcast.3132, ...), dimensions={0} | concatenate | bytes 1048576 | tf_op jit(solution)/shard_map/stack | solution.py:164
  145.7 1.9 %collective-permute-start.12 = (f32[4,1,1024]{2,1,0:T(1,128)S(1)}, f32[4,1,1024]{2,1,0:T(1,128)S(1)}, u32[]{:S(2)}, u32[]{:S(2)}) collective-permute-start(f32[4,1,1024]{2,1,0:T(1,128)S(1)} %pad_maximum_fusion.14), channel_id=1, source_target_pairs={{8,0},{16,8},{24,16},{32,24},{40,32},{48,40},{56,48},{64,56},{72,6... | collective-permute-start | bytes 49160 | tf_op jit(solution)/shard_map/ppermute | solution.py:12
  147.7 3.1 %collective-permute-done.12 = f32[4,1,1024]{2,1,0:T(1,128)S(1)} collective-permute-done((f32[4,1,1024]{2,1,0:T(1,128)S(1)}, f32[4,1,1024]{2,1,0:T(1,128)S(1)}, u32[]{:S(2)}, u32[]{:S(2)}) %collective-permute-start.12) | collective-permute-done | bytes 16416 | tf_op jit(solution)/shard_map/ppermute | solution.py:12
  150.8 1.1 multiply_subtract_fusion
  (530 shorter events, 17.4 us)
Async XLA Ops:
  0.0 13.3 %copy-start.1 = (f32[128,1024]{1,0:T(8,128)S(1)}, f32[128,1024]{1,0:T(8,128)}, u32[]{:S(2)}) copy-start(f32[128,1024]{1,0:T(8,128)} %param.6) | copy-start | bytes 1572868
  0.8 31.7 %collective-permute-start.1 = (f32[2,1024]{1,0:T(2,128)S(1)}, f32[2,1024]{1,0:T(2,128)S(1)}, u32[]{:S(2)}, u32[]{:S(2)}) collective-permute-start(f32[2,1024]{1,0:T(2,128)S(1)} %get-tuple-element.1839), channel_id=1, source_target_pairs={{8,0},{16,8},{24,16},{32,24},{40,32},{48,40},{56,48},{64,56},{72,6... | collective-permute-start | bytes 24584 | tf_op jit(solution)/shard_map/ppermute | solution.py:25
  6.0 26.6 %collective-permute-start = (f32[2,1024]{1,0:T(2,128)S(1)}, f32[2,1024]{1,0:T(2,128)S(1)}, u32[]{:S(2)}, u32[]{:S(2)}) collective-permute-start(f32[2,1024]{1,0:T(2,128)S(1)} %get-tuple-element.1840), channel_id=1, source_target_pairs={{0,8},{8,16},{16,24},{24,32},{32,40},{40,48},{48,56},{56,64},{64,7... | collective-permute-start | bytes 24584 | tf_op jit(solution)/shard_map/ppermute | solution.py:23
  7.9 5.6 %copy-start.2 = (f32[128,1024]{1,0:T(8,128)S(1)}, f32[128,1024]{1,0:T(8,128)}, u32[]{:S(2)}) copy-start(f32[128,1024]{1,0:T(8,128)} %param.7) | copy-start | bytes 1572868
  13.5 1.0 copy-start.4
  14.6 1.0 copy-start.3
  15.6 1.0 copy-start
  56.4 18.0 %collective-permute-start.3 = (f32[4,9,1024]{2,1,0:T(8,128)S(1)}, f32[4,9,1024]{2,1,0:T(8,128)S(1)}, u32[]{:S(2)}, u32[]{:S(2)}) collective-permute-start(f32[4,9,1024]{2,1,0:T(8,128)S(1)} %pad_maximum_fusion.1), channel_id=1, source_target_pairs={{0,8},{8,16},{16,24},{24,32},{32,40},{40,48},{48,56},{56,64},{64,7... | collective-permute-start | bytes 442376 | tf_op jit(solution)/shard_map/ppermute | solution.py:12
  58.3 16.1 %collective-permute-start.2 = (f32[4,9,1024]{2,1,0:T(8,128)S(1)}, f32[4,9,1024]{2,1,0:T(8,128)S(1)}, u32[]{:S(2)}, u32[]{:S(2)}) collective-permute-start(f32[4,9,1024]{2,1,0:T(8,128)S(1)} %pad_maximum_fusion.1), channel_id=1, source_target_pairs={{8,0},{16,8},{24,16},{32,24},{40,32},{48,40},{56,48},{64,56},{72,6... | collective-permute-start | bytes 442376 | tf_op jit(solution)/shard_map/ppermute | solution.py:12
  61.8 0.7 copy-start.119
  61.8 0.7 copy-start.120
  61.8 0.7 copy-start.121
  61.8 0.7 copy-start.122
  61.8 0.7 copy-start.86
  61.8 0.7 copy-start.87
  61.8 0.7 copy-start.88
  61.8 0.7 copy-start.89
  61.8 0.7 copy-start.90
  61.8 0.7 copy-start.91
  61.9 0.7 copy-start.92
  61.9 0.7 copy-start.93
  61.9 0.7 copy-start.94
  61.9 0.7 copy-start.95
  61.9 0.7 copy-start.96
  61.9 0.7 copy-start.97
  61.9 0.7 copy-start.98
  61.9 0.7 copy-start.99
  61.9 0.7 copy-start.100
  61.9 0.7 copy-start.101
  62.0 0.7 copy-start.108
  62.1 0.7 copy-start.83
  68.1 0.7 copy-start.52
  68.1 0.7 copy-start.53
  68.1 0.7 copy-start.54
  68.1 0.7 copy-start.59
  68.2 0.7 copy-start.64
  68.2 0.7 copy-start.66
  68.3 0.7 copy-start.79
  68.4 0.7 copy-start.45
  76.3 4.8 %collective-permute-start.5 = (f32[4,9,1024]{2,0,1:T(4,128)S(1)}, f32[4,9,1024]{2,0,1:T(4,128)S(1)}, u32[]{:S(2)}, u32[]{:S(2)}) collective-permute-start(f32[4,9,1024]{2,0,1:T(4,128)S(1)} %pad_maximum_fusion.3), channel_id=1, source_target_pairs={{0,16},{8,24},{16,32},{24,40},{32,48},{40,56},{48,64},{56,72},{64,... | collective-permute-start | bytes 442376 | tf_op jit(solution)/shard_map/ppermute | solution.py:12
  78.8 5.9 %collective-permute-start.4 = (f32[4,9,1024]{2,0,1:T(4,128)S(1)}, f32[4,9,1024]{2,0,1:T(4,128)S(1)}, u32[]{:S(2)}, u32[]{:S(2)}) collective-permute-start(f32[4,9,1024]{2,0,1:T(4,128)S(1)} %pad_maximum_fusion.3), channel_id=1, source_target_pairs={{16,0},{24,8},{32,16},{40,24},{48,32},{56,40},{64,48},{72,56},{80,... | collective-permute-start | bytes 442376 | tf_op jit(solution)/shard_map/ppermute | solution.py:12
  86.1 8.5 %collective-permute-start.7 = (f32[4,9,1024]{2,0,1:T(4,128)S(1)}, f32[4,9,1024]{2,0,1:T(4,128)S(1)}, u32[]{:S(2)}, u32[]{:S(2)}) collective-permute-start(f32[4,9,1024]{2,0,1:T(4,128)S(1)} %pad_maximum_fusion.5), channel_id=1, source_target_pairs={{0,32},{8,40},{16,48},{24,56},{32,64},{40,72},{48,80},{56,88},{64,... | collective-permute-start | bytes 442376 | tf_op jit(solution)/shard_map/ppermute | solution.py:12
  92.6 8.0 %collective-permute-start.6 = (f32[4,9,1024]{2,0,1:T(4,128)S(1)}, f32[4,9,1024]{2,0,1:T(4,128)S(1)}, u32[]{:S(2)}, u32[]{:S(2)}) collective-permute-start(f32[4,9,1024]{2,0,1:T(4,128)S(1)} %pad_maximum_fusion.5), channel_id=1, source_target_pairs={{32,0},{40,8},{48,16},{56,24},{64,32},{72,40},{80,48},{88,56},{96,... | collective-permute-start | bytes 442376 | tf_op jit(solution)/shard_map/ppermute | solution.py:12
  102.2 5.6 %collective-permute-start.9 = (f32[4,9,1024]{2,0,1:T(4,128)S(1)}, f32[4,9,1024]{2,0,1:T(4,128)S(1)}, u32[]{:S(2)}, u32[]{:S(2)}) collective-permute-start(f32[4,9,1024]{2,0,1:T(4,128)S(1)} %pad_maximum_fusion.7), channel_id=1, source_target_pairs={{0,64},{8,72},{16,80},{24,88},{32,96},{40,104},{48,112},{56,120},{... | collective-permute-start | bytes 442376 | tf_op jit(solution)/shard_map/ppermute | solution.py:12
  105.7 5.9 %collective-permute-start.8 = (f32[4,9,1024]{2,0,1:T(4,128)S(1)}, f32[4,9,1024]{2,0,1:T(4,128)S(1)}, u32[]{:S(2)}, u32[]{:S(2)}) collective-permute-start(f32[4,9,1024]{2,0,1:T(4,128)S(1)} %pad_maximum_fusion.7), channel_id=1, source_target_pairs={{64,0},{72,8},{80,16},{88,24},{96,32},{104,40},{112,48},{120,56},{... | collective-permute-start | bytes 442376 | tf_op jit(solution)/shard_map/ppermute | solution.py:12
  113.3 5.0 %collective-permute-start.11 = (f32[4,9,1024]{2,0,1:T(4,128)S(1)}, f32[4,9,1024]{2,0,1:T(4,128)S(1)}, u32[]{:S(2)}, u32[]{:S(2)}) collective-permute-start(f32[4,9,1024]{2,0,1:T(4,128)S(1)} %pad_maximum_fusion.9), channel_id=1, source_target_pairs={{0,128},{8,136},{16,144},{24,152},{32,160},{40,168},{48,176},{56,1... | collective-permute-start | bytes 442376 | tf_op jit(solution)/shard_map/ppermute | solution.py:12
  116.3 7.4 %collective-permute-start.10 = (f32[4,9,1024]{2,0,1:T(4,128)S(1)}, f32[4,9,1024]{2,0,1:T(4,128)S(1)}, u32[]{:S(2)}, u32[]{:S(2)}) collective-permute-start(f32[4,9,1024]{2,0,1:T(4,128)S(1)} %pad_maximum_fusion.9), channel_id=1, source_target_pairs={{128,0},{136,8},{144,16},{152,24},{160,32},{168,40},{176,48},{184,... | collective-permute-start | bytes 442376 | tf_op jit(solution)/shard_map/ppermute | solution.py:12
  124.9 22.8 %collective-permute-start.13 = (f32[4,1,1024]{2,1,0:T(1,128)S(1)}, f32[4,1,1024]{2,1,0:T(1,128)S(1)}, u32[]{:S(2)}, u32[]{:S(2)}) collective-permute-start(f32[4,1,1024]{2,1,0:T(1,128)S(1)} %pad_maximum_fusion.14), channel_id=1, source_target_pairs={{0,8},{8,16},{16,24},{24,32},{32,40},{40,48},{48,56},{56,64},{64,7... | collective-permute-start | bytes 49160 | tf_op jit(solution)/shard_map/ppermute | solution.py:12
  139.4 0.7 copy-start.13
  139.4 0.7 copy-start.14
  139.4 0.7 copy-start.15
  139.4 0.7 copy-start.16
  139.4 0.7 copy-start.17
  139.4 0.7 copy-start.18
  139.4 0.7 copy-start.19
  139.5 0.7 copy-start.20
  139.5 0.7 copy-start.21
  139.6 0.7 copy-start.31
  139.6 0.7 copy-start.34
  139.6 0.7 copy-start.35
  139.6 0.7 copy-start.37
  139.6 0.7 copy-start.38
  139.7 0.7 copy-start.5
  145.7 5.1 %collective-permute-start.12 = (f32[4,1,1024]{2,1,0:T(1,128)S(1)}, f32[4,1,1024]{2,1,0:T(1,128)S(1)}, u32[]{:S(2)}, u32[]{:S(2)}) collective-permute-start(f32[4,1,1024]{2,1,0:T(1,128)S(1)} %pad_maximum_fusion.14), channel_id=1, source_target_pairs={{8,0},{16,8},{24,16},{32,24},{40,32},{48,40},{56,48},{64,56},{72,6... | collective-permute-start | bytes 49160 | tf_op jit(solution)/shard_map/ppermute | solution.py:12
  (74 other events, 50.9 us)
where the time goes:
time: 154 us; the launch traced here: 152 us
  starting transfers between devices  47.5 us (31%)
  local copies, waits for them, and re-layouts  40.3 us (26%)
  other arithmetic  36.3 us (24%)
  waiting for transfers between devices  24.3 us (16%)
  between operations  3.49 us (2%)
    ppermute x12, starting transfers between devices, passed_along(): return lax.ppermute(array, axis, pairs)  40.5 us
    ppermute x12, waiting for transfers between devices, passed_along(): return lax.ppermute(array, axis, pairs)  24.3 us
    another operation x5, local copies, waits for them, and re-layouts, backward(): jnp.stack(items)  17.7 us
    sub x10, other arithmetic, solve_small(): rows_right[other_row] - factor * rows_right[pivot_col]  11.3 us
    sub x30, other arithmetic, solve_small(): rows_left[other_row] = rows_left[other_row] - factor * rows_left[pivot_col]  7.85 us
    sub x10, other arithmetic, backward(): factor_g[col_idx][step_idx] - factor_p[step_idx] * after_one[col_idx]  7.54 us
    slice x44, local copies, waits for them, and re-layouts, solve_small(): factor = rows_left[other_row][..., pivot_col:pivot_col + 1, :]  6.21 us
    slice x7, local copies, waits for them, and re-layouts, forward(): far_low[step_idx] * older_g[col_idx]  5.54 us
  transfers between devices with their start and end apart: 14, of which 9 were waited for; matrix products, arithmetic and copies ran while one was open for 27% of the time, Pallas kernels for 0%

commit v1 on v0

v1 whole, which is shorter than its diff:
```python
import jax
import jax.numpy as jnp
from jax import lax
from jax.experimental import pallas as pl
from jax.experimental.pallas import tpu as pltpu
from jax.sharding import PartitionSpec as P

ROWS = 128
SUBS = 4
CHUNKS = 4
TILE = (8, 128)
VMEM_BYTES = 12 << 20


def eliminate(state, coefs):
    (far_g, far_a, far_b, far_p, far_q), (near_g, near_a, near_b, near_p, near_q) = state
    low2, low1, up1, up2, target = coefs
    minus_diag = (((low2 + low1) + up1) + up2) - 1.0
    beta = low1 + low2 * far_p
    scale = pl.reciprocal(minus_diag - low2 * far_q - beta * near_p)
    new_g = (low2 * far_g + beta * near_g - target) * scale
    new_a = (low2 * far_a + beta * near_a) * scale
    new_b = (low2 * far_b + beta * near_b) * scale
    new_p = (up1 + beta * near_q) * scale
    new_q = up2 * scale
    return (new_g, new_a, new_b, new_p, new_q)


def eliminate_first(coefs):
    low2, low1, up1, up2, target = coefs
    scale = pl.reciprocal((((low2 + low1) + up1) + up2) - 1.0)
    return (-target * scale, low2 * scale, low1 * scale, up1 * scale, up2 * scale)


def eliminate_second(first, coefs):
    near_g, near_a, near_b, near_p, near_q = first
    low2, low1, up1, up2, target = coefs
    scale = pl.reciprocal((((low2 + low1) + up1) + up2) - 1.0 - low1 * near_p)
    return (
        (low1 * near_g - target) * scale,
        low1 * near_a * scale,
        (low2 + low1 * near_b) * scale,
        (up1 + low1 * near_q) * scale,
        up2 * scale,
    )


def carry_on(head, row):
    g, a, b, p, q = head
    row_g, row_a, row_b, row_p, row_q = row
    return (g + p * row_g, a + p * row_a, b + p * row_b, q + p * row_p, p * row_q)


def affine(row, w, e):
    return row[0] + row[1] * w[0] + row[2] * w[1] + row[3] * e[0] + row[4] * e[1]


def mix(row, left, right):
    return tuple(row[0] * x + row[1] * y for x, y in zip(left, right))


def split_of(first, second):
    r0, r1 = first[2], first[3]
    l0, l1 = second[0], second[1]
    n00 = r0[3] * l0[1] + r0[4] * l1[1]
    n01 = r0[3] * l0[2] + r0[4] * l1[2]
    n10 = r1[3] * l0[1] + r1[4] * l1[1]
    n11 = r1[3] * l0[2] + r1[4] * l1[2]
    d00 = 1.0 - n00
    d11 = 1.0 - n11
    inv = pl.reciprocal(d00 * d11 - n01 * n10)
    k0 = (d11 * inv, n01 * inv)
    k1 = (n10 * inv, d00 * inv)
    s0 = (r0[0] + r0[3] * l0[0] + r0[4] * l1[0], r0[1], r0[2]) + mix(r0[3:5], l0[3:5], l1[3:5])
    s1 = (r1[0] + r1[3] * l0[0] + r1[4] * l1[0], r1[1], r1[2]) + mix(r1[3:5], l0[3:5], l1[3:5])
    a0 = mix(k0, s0, s1)
    a1 = mix(k1, s0, s1)
    b0 = mix(l0[1:3], a0, a1)
    b1 = mix(l1[1:3], a0, a1)
    b0 = (b0[0] + l0[0], b0[1], b0[2], b0[3] + l0[3], b0[4] + l0[4])
    b1 = (b1[0] + l1[0], b1[1], b1[2], b1[3] + l1[3], b1[4] + l1[4])
    return (a0, a1, b0, b1)


def join(first, second, split):
    a0, a1, b0, b1 = split
    left, right = [], []
    for row in first[0:2]:
        far = mix(row[3:5], b0, b1)
        left.append((row[0] + far[0], row[1] + far[1], row[2] + far[2], far[3], far[4]))
    for row in second[2:4]:
        far = mix(row[1:3], a0, a1)
        right.append((row[0] + far[0], far[1], far[2], row[3] + far[3], row[4] + far[4]))
    return tuple(left + right)


def read_port(ref):
    return tuple(tuple(ref[5 * i + j] for j in range(5)) for i in range(4))


def write_port(ref, port):
    for i in range(4):
        for j in range(5):
            ref[5 * i + j] = port[i][j]


def swap_if(flag, one, two):
    first = tuple(tuple(jnp.where(flag, y, x) for x, y in zip(u, v)) for u, v in zip(one, two))
    second = tuple(tuple(jnp.where(flag, x, y) for x, y in zip(u, v)) for u, v in zip(one, two))
    return first, second


def row_of(buffers, sub, chunk, step):
    return tuple(buf[sub, chunk, pl.ds(step, 8, stride=8), :] for buf in buffers)


def port_kernel(*refs):
    sources, out, buffers, sems = refs[0:5], refs[5], refs[6:11], refs[11]
    copies = [
        [
            pltpu.make_async_copy(src.at[:, c], buf.at[:, c], sems.at[i, c])
            for i, (src, buf) in enumerate(zip(sources, buffers))
        ]
        for c in range(CHUNKS)
    ]
    for group in copies:
        for copy in group:
            copy.start()
    far, near = [None] * SUBS, [None] * SUBS
    head0, head1 = [None] * SUBS, [None] * SUBS
    for c in range(CHUNKS):
        for copy in copies[c]:
            copy.wait()
        for step in range(8):
            for s in range(SUBS):
                coefs = row_of(buffers, s, c, step)
                if c == 0 and step == 0:
                    near[s] = eliminate_first(coefs)
                    head0[s] = near[s]
                    continue
                if c == 0 and step == 1:
                    row = eliminate_second(near[s], coefs)
                    head1[s] = row
                else:
                    row = eliminate((far[s], near[s]), coefs)
                    head1[s] = carry_on(head1[s], row)
                head0[s] = carry_on(head0[s], row)
                far[s], near[s] = near[s], row
    ports = []
    for s in range(SUBS):
        g, a, b, p, q = far[s]
        row = near[s]
        tail0 = (g + p * row[0], a + p * row[1], b + p * row[2], q + p * row[3], p * row[4])
        ports.append((head0[s], head1[s], tail0, row))
    while len(ports) > 1:
        ports = [
            join(ports[i], ports[i + 1], split_of(ports[i], ports[i + 1]))
            for i in range(0, len(ports), 2)
        ]
    write_port(out, ports[0])


def spikes_kernel(l2, l1, u1, u2, tr, after, out, p_buf, q_buf):
    buffers = (l2, l1, u1, u2, tr)
    far, near = None, None
    for i in range(ROWS):
        coefs = row_of(buffers, i // 32, (i // 8) % 4, i % 8)
        if i == 0:
            row = eliminate_first(coefs)
        elif i == 1:
            row = eliminate_second(near, coefs)
        else:
            row = eliminate((far, near), coefs)
        out[0, i], out[1, i], out[2, i] = row[0], row[1], row[2]
        p_buf[i], q_buf[i] = row[3], row[4]
        far, near = near, row
    zero = jnp.zeros(TILE, jnp.float32)
    one = jnp.ones(TILE, jnp.float32)
    next1 = (zero, zero, zero, one, zero)
    next2 = (zero, zero, zero, zero, one)
    for i in reversed(range(ROWS)):
        p, q = p_buf[i], q_buf[i]
        own = mix((p, q), next1, next2)
        own = (own[0] + out[0, i], own[1] + out[1, i], own[2] + out[2, i], own[3], own[4])
        target = tr[i // 32, (i // 8) % 4, pl.ds(i % 8, 8, stride=8), :]
        out[0, i] = own[0] + own[0] - target
        for k in range(1, 5):
            out[k, i] = own[k]
        next2 = next1
        next1 = own


def core_kernel(own_ref, other_ref, out, split_out):
    is_high = lax.axis_index("lon") % 2 == 1
    first, second = swap_if(is_high, read_port(own_ref), read_port(other_ref))
    split = split_of(first, second)
    write_port(split_out, split)
    write_port(out, join(first, second, split))


def bits(divisor):
    place = (lax.axis_index("lon") // divisor) % 4
    return place % 2 == 1, place // 2 == 1


def group_kernel(own_ref, by1, by2, by3, out, split_pair, split_top):
    low_bit, high_bit = bits(2)
    first, second = swap_if(low_bit, read_port(own_ref), read_port(by1))
    split = split_of(first, second)
    write_port(split_pair, split)
    mine = join(first, second, split)
    first, second = swap_if(low_bit, read_port(by2), read_port(by3))
    theirs = join(first, second, split_of(first, second))
    first, second = swap_if(high_bit, mine, theirs)
    split = split_of(first, second)
    write_port(split_top, split)
    write_port(out, join(first, second, split))


def descend(flag, split, w, e):
    a0, a1 = affine(split[0], w, e), affine(split[1], w, e)
    b0, b1 = affine(split[2], w, e), affine(split[3], w, e)
    new_w = (jnp.where(flag, a0, w[0]), jnp.where(flag, a1, w[1]))
    new_e = (jnp.where(flag, e[0], b0), jnp.where(flag, e[1], b1))
    return new_w, new_e


def final_kernel(own_ref, by1, by2, by3, top_x, pair_x, core, spikes, out, stage, sems):
    low_bit, high_bit = bits(8)
    first, second = swap_if(low_bit, read_port(own_ref), read_port(by1))
    split_mine = split_of(first, second)
    mine = join(first, second, split_mine)
    first, second = swap_if(low_bit, read_port(by2), read_port(by3))
    theirs = join(first, second, split_of(first, second))
    first, second = swap_if(high_bit, mine, theirs)
    zero = jnp.zeros(TILE, jnp.float32)
    w, e = (zero, zero), (zero, zero)
    w, e = descend(high_bit, split_of(first, second), w, e)
    w, e = descend(low_bit, split_mine, w, e)
    low_bit, high_bit = bits(2)
    w, e = descend(high_bit, read_port(top_x), w, e)
    w, e = descend(low_bit, read_port(pair_x), w, e)
    w, e = descend(lax.axis_index("lon") % 2 == 1, read_port(core), w, e)
    weights = (w[0] + w[0], w[1] + w[1], e[0] + e[0], e[1] + e[1])
    copies = []
    for s in range(SUBS):
        for c in range(CHUNKS):
            for step in range(8):
                i = 32 * s + 8 * c + step
                value = spikes[0, i]
                for k in range(4):
                    value = value + spikes[k + 1, i] * weights[k]
                stage[s, c, pl.ds(step, 8, stride=8), :] = value
        copy = pltpu.make_async_copy(stage.at[s], out.at[s], sems.at[s])
        copy.start()
        copies.append(copy)
    for copy in copies:
        copy.wait()


def call(kernel, outs, operands, out_specs=None, in_specs=None, scratch=(), name=None):
    vmem = pl.BlockSpec(memory_space=pltpu.VMEM)
    return pl.pallas_call(
        kernel,
        out_shape=[jax.ShapeDtypeStruct(shape, jnp.float32) for shape in outs],
        in_specs=in_specs or [vmem] * len(operands),
        out_specs=out_specs or [vmem] * len(outs),
        scratch_shapes=list(scratch),
        compiler_params=pltpu.CompilerParams(vmem_limit_bytes=VMEM_BYTES),
        name=name,
    )(*operands)


def exchange(port, bit_mask):
    return lax.ppermute(port, "lon", [(i, i ^ bit_mask) for i in range(32)])


def per_device(tracer, lower2, lower1, upper1, upper2):
    vmem = pl.BlockSpec(memory_space=pltpu.VMEM)
    hbm = pl.BlockSpec(memory_space=pltpu.HBM)
    tiles = (SUBS, CHUNKS, 64, 128)

    def view(array):
        return array.reshape(16, 8, 8, 128).transpose(0, 2, 1, 3).reshape(tiles)

    arrays = [
        pltpu.with_memory_space_constraint(view(a), pltpu.HBM)
        for a in (lower2, lower1, upper1, upper2, tracer)
    ]
    port_shape = (20,) + TILE
    port, *loaded = call(
        port_kernel,
        [port_shape] + [tiles] * 5,
        arrays,
        in_specs=[hbm] * 5,
        scratch=[pltpu.SemaphoreType.DMA((5, CHUNKS))],
        name="segment_port",
    )
    chip, core_split = call(core_kernel, [port_shape] * 2, [port, exchange(port, 1)], name="core_join")
    by_x = [exchange(chip, k) for k in (2, 4, 6)]
    (spikes,) = call(
        spikes_kernel,
        [(5, ROWS) + TILE],
        loaded + [chip],
        scratch=[pltpu.VMEM((ROWS,) + TILE, jnp.float32)] * 2,
        name="segment_spikes",
    )
    group, pair_x, top_x = call(group_kernel, [port_shape] * 3, [chip] + by_x, name="x_join")
    by_y = [exchange(group, k) for k in (8, 16, 24)]
    (out,) = call(
        final_kernel,
        [tiles],
        [group] + by_y + [top_x, pair_x, core_split, spikes],
        out_specs=[hbm],
        scratch=[pltpu.VMEM(tiles, jnp.float32), pltpu.SemaphoreType.DMA((SUBS,))],
        name="combine",
    )
    return out.reshape(16, 8, 8, 128).transpose(0, 2, 1, 3).reshape(ROWS, 1024)


def solution(mesh):
    spec = P("lon", "lat")
    return jax.shard_map(
        per_device, mesh=mesh, in_specs=(spec,) * 5, out_specs=spec, check_vma=False
    )
```

time: 154 us -> 23.6 us (0.15)
  the two profiles are of different devices: /device:TPU:1 before, /device:TPU:128 now
where the time goes in v1:
time: 23.6 us; the launch traced here: 23.5 us
  waiting for transfers between devices  9.83 us (42%)
  starting transfers between devices  8.46 us (36%)
  Pallas kernels  5.19 us (22%)
    ppermute x7, waiting for transfers between devices, exchange(): return lax.ppermute(port, 'lon', [(i, i ^ bit_mask) for i in range(32)])  9.83 us
    ppermute x7, starting transfers between devices, exchange(): return lax.ppermute(port, 'lon', [(i, i ^ bit_mask) for i in range(32)])  8.46 us
    pallas_call x5, Pallas kernels, call(): pl.pallas_call(kernel, out_shape=[jax.ShapeDtypeStruct(shape, jnp.float32...  5.19 us
  transfers between devices with their start and end apart: 7, of which 5 were waited for; matrix products, arithmetic and copies ran while one was open for 0% of the time, Pallas kernels for 7%

profile of v1, /device:TPU:128, one launch (start us, length us, event | category | flops | bytes accessed | tf_op | source)
XLA Modules:
  0.0 23.5 jit_solution(15910730859655932649)
XLA Ops:
  0.0 2.5 %segment_port.1 = (f32[20,8,128]{2,1,0:T(8,128)S(1)}, f32[4,4,64,128]{3,2,1,0:T(8,128)S(1)}, f32[4,4,64,128]{3,2,1,0:T(8,128)S(1)}, f32[4,4,64,128]{3,2,1,0:T(8,...) custom-call(f32[4,4,64,128]{3,2,1,0:T(8,128)} %bitcast.30, f32[4,4,64,128]{3,2,1,0:T(8,128)} %bitcast.31, ...), custom_call_target="tpu_custom_call" | custom-call | tf_op jit(solution)/shard_map/segment_port/pallas_call | solution.py:263
  2.5 0.1 collective-permute-start
  2.6 1.3 %collective-permute-done.other_ref = f32[20,8,128]{2,1,0:T(8,128)S(1)} collective-permute-done((f32[20,8,128]{2,1,0:T(8,128)S(1)}, f32[20,8,128]{2,1,0:T(8,128)S(1)}, u32[]{:S(2)}, u32[]{:S(2)}) %collective-permute-start) | collective-permute-done | bytes 81952 | tf_op jit(solution)/shard_map/ppermute | solution.py:275
  3.9 2.8 %collective-permute-start.3 = (f32[20,8,128]{2,1,0:T(8,128)S(1)}, f32[20,8,128]{2,1,0:T(8,128)S(1)}, u32[]{:S(2)}, u32[]{:S(2)}) collective-permute-start(f32[20,8,128]{2,1,0:T(8,128)S(1)} %get-tuple-element.17.own_ref.after), channel_id=1, source_target_pairs={{0,48},{8,56},{16,32},{24,40},{32,16},{40,24},{48,0},{56,8},{64,11... | collective-permute-start | bytes 245768 | tf_op jit(solution)/shard_map/ppermute | solution.py:275
  6.7 0.8 %collective-permute-start.2 = (f32[20,8,128]{2,1,0:T(8,128)S(1)}, f32[20,8,128]{2,1,0:T(8,128)S(1)}, u32[]{:S(2)}, u32[]{:S(2)}) collective-permute-start(f32[20,8,128]{2,1,0:T(8,128)S(1)} %get-tuple-element.17.own_ref.after), channel_id=1, source_target_pairs={{0,32},{8,40},{16,48},{24,56},{32,0},{40,8},{48,16},{56,24},{64,96... | collective-permute-start | bytes 245768 | tf_op jit(solution)/shard_map/ppermute | solution.py:275
  7.5 0.5 %collective-permute-start.1 = (f32[20,8,128]{2,1,0:T(8,128)S(1)}, f32[20,8,128]{2,1,0:T(8,128)S(1)}, u32[]{:S(2)}, u32[]{:S(2)}) collective-permute-start(f32[20,8,128]{2,1,0:T(8,128)S(1)} %get-tuple-element.17.own_ref.after), channel_id=1, source_target_pairs={{0,16},{8,24},{16,0},{24,8},{32,48},{40,56},{48,32},{56,40},{64,80... | collective-permute-start | bytes 245768 | tf_op jit(solution)/shard_map/ppermute | solution.py:275
  8.1 2.5 %collective-permute-done.3.by3 = f32[20,8,128]{2,1,0:T(8,128)S(1)} collective-permute-done((f32[20,8,128]{2,1,0:T(8,128)S(1)}, f32[20,8,128]{2,1,0:T(8,128)S(1)}, u32[]{:S(2)}, u32[]{:S(2)}) %collective-permute-start.3) | collective-permute-done | bytes 81952 | tf_op jit(solution)/shard_map/ppermute | solution.py:275
  10.5 2.8 %collective-permute-done.2.by2 = f32[20,8,128]{2,1,0:T(8,128)S(1)} collective-permute-done((f32[20,8,128]{2,1,0:T(8,128)S(1)}, f32[20,8,128]{2,1,0:T(8,128)S(1)}, u32[]{:S(2)}, u32[]{:S(2)}) %collective-permute-start.2) | collective-permute-done | bytes 81952 | tf_op jit(solution)/shard_map/ppermute | solution.py:275
  13.3 0.0 collective-permute-done.1.by1
  13.3 0.1 x_join.1
  13.5 3.1 %collective-permute-start.6 = (f32[20,8,128]{2,1,0:T(8,128)S(1)}, f32[20,8,128]{2,1,0:T(8,128)S(1)}, u32[]{:S(2)}, u32[]{:S(2)}) collective-permute-start(f32[20,8,128]{2,1,0:T(8,128)S(1)} %get-tuple-element.18.own_ref), channel_id=1, source_target_pairs={{0,192},{8,200},{16,208},{24,216},{32,224},{40,232},{48,240},{56,2... | collective-permute-start | bytes 245768 | tf_op jit(solution)/shard_map/ppermute | solution.py:275
  16.6 0.6 %collective-permute-start.5 = (f32[20,8,128]{2,1,0:T(8,128)S(1)}, f32[20,8,128]{2,1,0:T(8,128)S(1)}, u32[]{:S(2)}, u32[]{:S(2)}) collective-permute-start(f32[20,8,128]{2,1,0:T(8,128)S(1)} %get-tuple-element.18.own_ref), channel_id=1, source_target_pairs={{0,128},{8,136},{16,144},{24,152},{32,160},{40,168},{48,176},{56,1... | collective-permute-start | bytes 245768 | tf_op jit(solution)/shard_map/ppermute | solution.py:275
  17.2 0.5 %collective-permute-start.4 = (f32[20,8,128]{2,1,0:T(8,128)S(1)}, f32[20,8,128]{2,1,0:T(8,128)S(1)}, u32[]{:S(2)}, u32[]{:S(2)}) collective-permute-start(f32[20,8,128]{2,1,0:T(8,128)S(1)} %get-tuple-element.18.own_ref), channel_id=1, source_target_pairs={{0,64},{8,72},{16,80},{24,88},{32,96},{40,104},{48,112},{56,120},{... | collective-permute-start | bytes 245768 | tf_op jit(solution)/shard_map/ppermute | solution.py:275
  17.7 1.6 %segment_spikes.1.spikes = f32[5,128,8,128]{3,2,1,0:T(8,128)S(1)} custom-call(f32[4,4,64,128]{3,2,1,0:T(8,128)S(1)} %get-tuple-element.22.l2, f32[4,4,64,128]{3,2,1,0:T(8,128)S(1)} %get-tuple-element.23.l1, f32[4,4,64,128]{3,2,1,0:T(8,128)S(1)} %get-tuple-element.24.u1, f32[4,4,64,128]{3,2,1,0:T(8,128)S(1)} %get-tuple-element.25.u2, ...), custom_call_target="tpu_custom_call" | custom-call | tf_op jit(solution)/shard_map/segment_spikes/pallas_call | solution.py:263
  19.2 0.9 %collective-permute-done.6.by3 = f32[20,8,128]{2,1,0:T(8,128)S(1)} collective-permute-done((f32[20,8,128]{2,1,0:T(8,128)S(1)}, f32[20,8,128]{2,1,0:T(8,128)S(1)}, u32[]{:S(2)}, u32[]{:S(2)}) %collective-permute-start.6) | collective-permute-done | bytes 81952 | tf_op jit(solution)/shard_map/ppermute | solution.py:275
  20.1 2.4 %collective-permute-done.5.by2 = f32[20,8,128]{2,1,0:T(8,128)S(1)} collective-permute-done((f32[20,8,128]{2,1,0:T(8,128)S(1)}, f32[20,8,128]{2,1,0:T(8,128)S(1)}, u32[]{:S(2)}, u32[]{:S(2)}) %collective-permute-start.5) | collective-permute-done | bytes 81952 | tf_op jit(solution)/shard_map/ppermute | solution.py:275
  22.5 0.0 collective-permute-done.4.by1
  22.5 1.0 %combine.1 = f32[4,4,64,128]{3,2,1,0:T(8,128)} custom-call(f32[20,8,128]{2,1,0:T(8,128)S(1)} %get-tuple-element.18.own_ref, f32[20,8,128]{2,1,0:T(8,128)S(1)} %collective-permute-done.4.by1, f32[20,8,128]{2,1,0:T(8,128)S(1)} %collective-permute-done.5.by2, f32[20,8,128]{2,1,0:T(8,128)S(1)} %collective-permute-done.6.by3, ...), custom_call_target="tpu_custom_call" | custom-call | tf_op jit(solution)/shard_map/combine/pallas_call | solution.py:263
  (1 shorter events, 0.0 us)
Async XLA Ops:
  2.5 1.4 %collective-permute-start = (f32[20,8,128]{2,1,0:T(8,128)S(1)}, f32[20,8,128]{2,1,0:T(8,128)S(1)}, u32[]{:S(2)}, u32[]{:S(2)}) collective-permute-start(f32[20,8,128]{2,1,0:T(8,128)S(1)} %get-tuple-element.16.own_ref), channel_id=1, source_target_pairs={{0,8},{8,0},{16,24},{24,16},{32,40},{40,32},{48,56},{56,48},{64,72... | collective-permute-start | bytes 245768 | tf_op jit(solution)/shard_map/ppermute | solution.py:275
  3.9 6.7 %collective-permute-start.3 = (f32[20,8,128]{2,1,0:T(8,128)S(1)}, f32[20,8,128]{2,1,0:T(8,128)S(1)}, u32[]{:S(2)}, u32[]{:S(2)}) collective-permute-start(f32[20,8,128]{2,1,0:T(8,128)S(1)} %get-tuple-element.17.own_ref.after), channel_id=1, source_target_pairs={{0,48},{8,56},{16,32},{24,40},{32,16},{40,24},{48,0},{56,8},{64,11... | collective-permute-start | bytes 245768 | tf_op jit(solution)/shard_map/ppermute | solution.py:275
  6.7 6.6 %collective-permute-start.2 = (f32[20,8,128]{2,1,0:T(8,128)S(1)}, f32[20,8,128]{2,1,0:T(8,128)S(1)}, u32[]{:S(2)}, u32[]{:S(2)}) collective-permute-start(f32[20,8,128]{2,1,0:T(8,128)S(1)} %get-tuple-element.17.own_ref.after), channel_id=1, source_target_pairs={{0,32},{8,40},{16,48},{24,56},{32,0},{40,8},{48,16},{56,24},{64,96... | collective-permute-start | bytes 245768 | tf_op jit(solution)/shard_map/ppermute | solution.py:275
  7.5 5.8 %collective-permute-start.1 = (f32[20,8,128]{2,1,0:T(8,128)S(1)}, f32[20,8,128]{2,1,0:T(8,128)S(1)}, u32[]{:S(2)}, u32[]{:S(2)}) collective-permute-start(f32[20,8,128]{2,1,0:T(8,128)S(1)} %get-tuple-element.17.own_ref.after), channel_id=1, source_target_pairs={{0,16},{8,24},{16,0},{24,8},{32,48},{40,56},{48,32},{56,40},{64,80... | collective-permute-start | bytes 245768 | tf_op jit(solution)/shard_map/ppermute | solution.py:275
  13.5 6.6 %collective-permute-start.6 = (f32[20,8,128]{2,1,0:T(8,128)S(1)}, f32[20,8,128]{2,1,0:T(8,128)S(1)}, u32[]{:S(2)}, u32[]{:S(2)}) collective-permute-start(f32[20,8,128]{2,1,0:T(8,128)S(1)} %get-tuple-element.18.own_ref), channel_id=1, source_target_pairs={{0,192},{8,200},{16,208},{24,216},{32,224},{40,232},{48,240},{56,2... | collective-permute-start | bytes 245768 | tf_op jit(solution)/shard_map/ppermute | solution.py:275
  16.6 5.9 %collective-permute-start.5 = (f32[20,8,128]{2,1,0:T(8,128)S(1)}, f32[20,8,128]{2,1,0:T(8,128)S(1)}, u32[]{:S(2)}, u32[]{:S(2)}) collective-permute-start(f32[20,8,128]{2,1,0:T(8,128)S(1)} %get-tuple-element.18.own_ref), channel_id=1, source_target_pairs={{0,128},{8,136},{16,144},{24,152},{32,160},{40,168},{48,176},{56,1... | collective-permute-start | bytes 245768 | tf_op jit(solution)/shard_map/ppermute | solution.py:275
  17.2 5.3 %collective-permute-start.4 = (f32[20,8,128]{2,1,0:T(8,128)S(1)}, f32[20,8,128]{2,1,0:T(8,128)S(1)}, u32[]{:S(2)}, u32[]{:S(2)}) collective-permute-start(f32[20,8,128]{2,1,0:T(8,128)S(1)} %get-tuple-element.18.own_ref), channel_id=1, source_target_pairs={{0,64},{8,72},{16,80},{24,88},{32,96},{40,104},{48,112},{56,120},{... | collective-permute-start | bytes 245768 | tf_op jit(solution)/shard_map/ppermute | solution.py:275

commit v2 on v1

--- a/solution.py
+++ b/solution.py
@@ -225,7 +225,7 @@
     return new_w, new_e
 
 
-def final_kernel(own_ref, by1, by2, by3, top_x, pair_x, core, spikes, out, stage, sems):
+def solve_kernel(own_ref, by1, by2, by3, top_x, pair_x, core, before, low_out, high_out):
     low_bit, high_bit = bits(8)
     first, second = swap_if(low_bit, read_port(own_ref), read_port(by1))
     split_mine = split_of(first, second)
@@ -240,8 +240,16 @@
     low_bit, high_bit = bits(2)
     w, e = descend(high_bit, read_port(top_x), w, e)
     w, e = descend(low_bit, read_port(pair_x), w, e)
-    w, e = descend(lax.axis_index("lon") % 2 == 1, read_port(core), w, e)
-    weights = (w[0] + w[0], w[1] + w[1], e[0] + e[0], e[1] + e[1])
+    a0, a1, b0, b1 = (affine(row, w, e) for row in read_port(core))
+    for k, value in enumerate((w[0], w[1], b0, b1)):
+        low_out[k] = value + value
+    for k, value in enumerate((a0, a1, e[0], e[1])):
+        high_out[k] = value + value
+
+
+def combine_kernel(received, high_own, spikes, out, stage, sems):
+    is_high = lax.axis_index("lon") % 2 == 1
+    weights = [jnp.where(is_high, high_own[k], received[k]) for k in range(4)]
     copies = []
     for s in range(SUBS):
         for c in range(CHUNKS):
@@ -271,8 +279,9 @@
     )(*operands)
 
 
-def exchange(port, bit_mask):
-    return lax.ppermute(port, "lon", [(i, i ^ bit_mask) for i in range(32)])
+def exchange(port, odd_mask, even_mask):
+    pairs = [(i, i ^ (odd_mask if i % 2 else even_mask)) for i in range(32)]
+    return lax.ppermute(port, "lon", pairs)
 
 
 def per_device(tracer, lower2, lower1, upper1, upper2):
@@ -296,8 +305,10 @@
         scratch=[pltpu.SemaphoreType.DMA((5, CHUNKS))],
         name="segment_port",
     )
-    chip, core_split = call(core_kernel, [port_shape] * 2, [port, exchange(port, 1)], name="core_join")
-    by_x = [exchange(chip, k) for k in (2, 4, 6)]
+    chip, core_split = call(
+        core_kernel, [port_shape] * 2, [port, exchange(port, 1, 1)], name="core_join"
+    )
+    by_x = [exchange(chip, k, 8) for k in (2, 4, 6)]
     (spikes,) = call(
         spikes_kernel,
         [(5, ROWS) + TILE],
@@ -306,11 +317,17 @@
         name="segment_spikes",
     )
     group, pair_x, top_x = call(group_kernel, [port_shape] * 3, [chip] + by_x, name="x_join")
-    by_y = [exchange(group, k) for k in (8, 16, 24)]
+    by_y = [exchange(group, k, 2) for k in (8, 16, 24)]
+    low_ends, high_ends = call(
+        solve_kernel,
+        [(4,) + TILE] * 2,
+        [group] + by_y + [top_x, pair_x, core_split, spikes],
+        name="y_solve",
+    )
     (out,) = call(
-        final_kernel,
+        combine_kernel,
         [tiles],
-        [group] + by_y + [top_x, pair_x, core_split, spikes],
+        [exchange(low_ends, 1, 1), high_ends, spikes],
         out_specs=[hbm],
         scratch=[pltpu.VMEM(tiles, jnp.float32), pltpu.SemaphoreType.DMA((SUBS,))],
         name="combine",

time: 23.6 us -> 22.5 us (0.953)
  the two profiles are of different devices: /device:TPU:128 before, /device:TPU:1 now
where the time goes in v2:
time: 22.5 us; the launch traced here: 22.4 us
  starting transfers between devices  10.3 us (46%)
  waiting for transfers between devices  6.88 us (31%)
  Pallas kernels  5.2 us (23%)
    ppermute x8, starting transfers between devices, exchange(): return lax.ppermute(port, 'lon', pairs)  10.3 us
    ppermute x8, waiting for transfers between devices, exchange(): return lax.ppermute(port, 'lon', pairs)  6.88 us
    pallas_call x6, Pallas kernels, call(): pl.pallas_call(kernel, out_shape=[jax.ShapeDtypeStruct(shape, jnp.float32...  5.2 us
  transfers between devices with their start and end apart: 8, of which 6 were waited for; matrix products, arithmetic and copies ran while one was open for 0% of the time, Pallas kernels for 7%

profile of v2, /device:TPU:1, one launch (start us, length us, event | category | flops | bytes accessed | tf_op | source)
XLA Modules:
  0.0 22.4 jit_solution(8859493761579806321)
XLA Ops:
  0.0 2.5 %segment_port.1 = (f32[20,8,128]{2,1,0:T(8,128)S(1)}, f32[4,4,64,128]{3,2,1,0:T(8,128)S(1)}, f32[4,4,64,128]{3,2,1,0:T(8,128)S(1)}, f32[4,4,64,128]{3,2,1,0:T(8,...) custom-call(f32[4,4,64,128]{3,2,1,0:T(8,128)} %bitcast.30, f32[4,4,64,128]{3,2,1,0:T(8,128)} %bitcast.31, ...), custom_call_target="tpu_custom_call" | custom-call | tf_op jit(solution)/shard_map/segment_port/pallas_call | solution.py:271
  2.5 3.3 %collective-permute-start = (f32[20,8,128]{2,1,0:T(8,128)S(1)}, f32[20,8,128]{2,1,0:T(8,128)S(1)}, u32[]{:S(2)}, u32[]{:S(2)}) collective-permute-start(f32[20,8,128]{2,1,0:T(8,128)S(1)} %get-tuple-element.18.own_ref), channel_id=1, source_target_pairs={{0,8},{8,0},{16,24},{24,16},{32,40},{40,32},{48,56},{56,48},{64,72... | collective-permute-start | bytes 245768 | tf_op jit(solution)/shard_map/ppermute | solution.py:284
  5.8 0.9 %collective-permute-done.other_ref = f32[20,8,128]{2,1,0:T(8,128)S(1)} collective-permute-done((f32[20,8,128]{2,1,0:T(8,128)S(1)}, f32[20,8,128]{2,1,0:T(8,128)S(1)}, u32[]{:S(2)}, u32[]{:S(2)}) %collective-permute-start) | collective-permute-done | bytes 81952 | tf_op jit(solution)/shard_map/ppermute | solution.py:284
  6.8 0.8 %collective-permute-start.3 = (f32[20,8,128]{2,1,0:T(8,128)S(1)}, f32[20,8,128]{2,1,0:T(8,128)S(1)}, u32[]{:S(2)}, u32[]{:S(2)}) collective-permute-start(f32[20,8,128]{2,1,0:T(8,128)S(1)} %get-tuple-element.19.own_ref.after), channel_id=1, source_target_pairs={{0,64},{8,56},{16,80},{24,40},{32,96},{40,24},{48,112},{56,8},{64,... | collective-permute-start | bytes 245768 | tf_op jit(solution)/shard_map/ppermute | solution.py:284
  7.6 0.5 %collective-permute-start.2 = (f32[20,8,128]{2,1,0:T(8,128)S(1)}, f32[20,8,128]{2,1,0:T(8,128)S(1)}, u32[]{:S(2)}, u32[]{:S(2)}) collective-permute-start(f32[20,8,128]{2,1,0:T(8,128)S(1)} %get-tuple-element.19.own_ref.after), channel_id=1, source_target_pairs={{0,64},{8,40},{16,80},{24,56},{32,96},{40,8},{48,112},{56,24},{64,... | collective-permute-start | bytes 245768 | tf_op jit(solution)/shard_map/ppermute | solution.py:284
  8.1 2.0 %collective-permute-start.1 = (f32[20,8,128]{2,1,0:T(8,128)S(1)}, f32[20,8,128]{2,1,0:T(8,128)S(1)}, u32[]{:S(2)}, u32[]{:S(2)}) collective-permute-start(f32[20,8,128]{2,1,0:T(8,128)S(1)} %get-tuple-element.19.own_ref.after), channel_id=1, source_target_pairs={{0,64},{8,24},{16,80},{24,8},{32,96},{40,56},{48,112},{56,40},{64,... | collective-permute-start | bytes 245768 | tf_op jit(solution)/shard_map/ppermute | solution.py:284
  10.1 1.2 %collective-permute-done.3.by3 = f32[20,8,128]{2,1,0:T(8,128)S(1)} collective-permute-done((f32[20,8,128]{2,1,0:T(8,128)S(1)}, f32[20,8,128]{2,1,0:T(8,128)S(1)}, u32[]{:S(2)}, u32[]{:S(2)}) %collective-permute-start.3) | collective-permute-done | bytes 81952 | tf_op jit(solution)/shard_map/ppermute | solution.py:284
  11.4 1.0 %collective-permute-done.2.by2 = f32[20,8,128]{2,1,0:T(8,128)S(1)} collective-permute-done((f32[20,8,128]{2,1,0:T(8,128)S(1)}, f32[20,8,128]{2,1,0:T(8,128)S(1)}, u32[]{:S(2)}, u32[]{:S(2)}) %collective-permute-start.2) | collective-permute-done | bytes 81952 | tf_op jit(solution)/shard_map/ppermute | solution.py:284
  12.4 0.7 %collective-permute-done.1.by1 = f32[20,8,128]{2,1,0:T(8,128)S(1)} collective-permute-done((f32[20,8,128]{2,1,0:T(8,128)S(1)}, f32[20,8,128]{2,1,0:T(8,128)S(1)}, u32[]{:S(2)}, u32[]{:S(2)}) %collective-permute-start.1) | collective-permute-done | bytes 81952 | tf_op jit(solution)/shard_map/ppermute | solution.py:284
  13.1 0.1 x_join.1
  13.2 2.1 %collective-permute-start.6 = (f32[20,8,128]{2,1,0:T(8,128)S(1)}, f32[20,8,128]{2,1,0:T(8,128)S(1)}, u32[]{:S(2)}, u32[]{:S(2)}) collective-permute-start(f32[20,8,128]{2,1,0:T(8,128)S(1)} %get-tuple-element.20.own_ref), channel_id=1, source_target_pairs={{0,16},{8,200},{16,0},{24,216},{32,48},{40,232},{48,32},{56,248},{... | collective-permute-start | bytes 245768 | tf_op jit(solution)/shard_map/ppermute | solution.py:284
  15.4 0.3 %collective-permute-start.5 = (f32[20,8,128]{2,1,0:T(8,128)S(1)}, f32[20,8,128]{2,1,0:T(8,128)S(1)}, u32[]{:S(2)}, u32[]{:S(2)}) collective-permute-start(f32[20,8,128]{2,1,0:T(8,128)S(1)} %get-tuple-element.20.own_ref), channel_id=1, source_target_pairs={{0,16},{8,136},{16,0},{24,152},{32,48},{40,168},{48,32},{56,184},{... | collective-permute-start | bytes 245768 | tf_op jit(solution)/shard_map/ppermute | solution.py:284
  15.7 0.9 %collective-permute-start.4 = (f32[20,8,128]{2,1,0:T(8,128)S(1)}, f32[20,8,128]{2,1,0:T(8,128)S(1)}, u32[]{:S(2)}, u32[]{:S(2)}) collective-permute-start(f32[20,8,128]{2,1,0:T(8,128)S(1)} %get-tuple-element.20.own_ref), channel_id=1, source_target_pairs={{0,16},{8,72},{16,0},{24,88},{32,48},{40,104},{48,32},{56,120},{64... | collective-permute-start | bytes 245768 | tf_op jit(solution)/shard_map/ppermute | solution.py:284
  16.6 1.6 %segment_spikes.1.before.spikes = f32[5,128,8,128]{3,2,1,0:T(8,128)S(1)} custom-call(f32[4,4,64,128]{3,2,1,0:T(8,128)S(1)} %get-tuple-element.24.l2, f32[4,4,64,128]{3,2,1,0:T(8,128)S(1)} %get-tuple-element.25.l1, f32[4,4,64,128]{3,2,1,0:T(8,128)S(1)} %get-tuple-element.26.u1, f32[4,4,64,128]{3,2,1,0:T(8,128)S(1)} %get-tuple-element.27.u2, ...), custom_call_target="tpu_custom_call" | custom-call | tf_op jit(solution)/shard_map/segment_spikes/pallas_call | solution.py:271
  18.2 0.0 collective-permute-done.6.by3
  18.2 2.0 %collective-permute-done.5.by2 = f32[20,8,128]{2,1,0:T(8,128)S(1)} collective-permute-done((f32[20,8,128]{2,1,0:T(8,128)S(1)}, f32[20,8,128]{2,1,0:T(8,128)S(1)}, u32[]{:S(2)}, u32[]{:S(2)}) %collective-permute-start.5) | collective-permute-done | bytes 81952 | tf_op jit(solution)/shard_map/ppermute | solution.py:284
  20.1 0.0 collective-permute-done.4.by1
  20.2 0.1 y_solve.1
  20.3 0.3 %collective-permute-start.7 = (f32[4,8,128]{2,1,0:T(8,128)S(1)}, f32[4,8,128]{2,1,0:T(8,128)S(1)}, u32[]{:S(2)}, u32[]{:S(2)}) collective-permute-start(f32[4,8,128]{2,1,0:T(8,128)S(1)} %get-tuple-element.29), channel_id=1, source_target_pairs={{0,8},{8,0},{16,24},{24,16},{32,40},{40,32},{48,56},{56,48},{64,72... | collective-permute-start | bytes 49160 | tf_op jit(solution)/shard_map/ppermute | solution.py:284
  20.6 1.0 %collective-permute-done.7.received = f32[4,8,128]{2,1,0:T(8,128)S(1)} collective-permute-done((f32[4,8,128]{2,1,0:T(8,128)S(1)}, f32[4,8,128]{2,1,0:T(8,128)S(1)}, u32[]{:S(2)}, u32[]{:S(2)}) %collective-permute-start.7) | collective-permute-done | bytes 16416 | tf_op jit(solution)/shard_map/ppermute | solution.py:284
  21.6 0.9 %combine.1 = f32[4,4,64,128]{3,2,1,0:T(8,128)} custom-call(f32[4,8,128]{2,1,0:T(8,128)S(1)} %collective-permute-done.7.received, f32[4,8,128]{2,1,0:T(8,128)S(1)} %get-tuple-element.30.high_own, f32[5,128,8,128]{3,2,1,0:T(8,128)S(1)} %segment_spikes.1.before.spikes), custom_call_target="tpu_custom_call" | custom-call | tf_op jit(solution)/shard_map/combine/pallas_call | solution.py:271
  (1 shorter events, 0.0 us)
Async XLA Ops:
  2.5 4.3 %collective-permute-start = (f32[20,8,128]{2,1,0:T(8,128)S(1)}, f32[20,8,128]{2,1,0:T(8,128)S(1)}, u32[]{:S(2)}, u32[]{:S(2)}) collective-permute-start(f32[20,8,128]{2,1,0:T(8,128)S(1)} %get-tuple-element.18.own_ref), channel_id=1, source_target_pairs={{0,8},{8,0},{16,24},{24,16},{32,40},{40,32},{48,56},{56,48},{64,72... | collective-permute-start | bytes 245768 | tf_op jit(solution)/shard_map/ppermute | solution.py:284
  6.8 4.6 %collective-permute-start.3 = (f32[20,8,128]{2,1,0:T(8,128)S(1)}, f32[20,8,128]{2,1,0:T(8,128)S(1)}, u32[]{:S(2)}, u32[]{:S(2)}) collective-permute-start(f32[20,8,128]{2,1,0:T(8,128)S(1)} %get-tuple-element.19.own_ref.after), channel_id=1, source_target_pairs={{0,64},{8,56},{16,80},{24,40},{32,96},{40,24},{48,112},{56,8},{64,... | collective-permute-start | bytes 245768 | tf_op jit(solution)/shard_map/ppermute | solution.py:284
  7.6 4.8 %collective-permute-start.2 = (f32[20,8,128]{2,1,0:T(8,128)S(1)}, f32[20,8,128]{2,1,0:T(8,128)S(1)}, u32[]{:S(2)}, u32[]{:S(2)}) collective-permute-start(f32[20,8,128]{2,1,0:T(8,128)S(1)} %get-tuple-element.19.own_ref.after), channel_id=1, source_target_pairs={{0,64},{8,40},{16,80},{24,56},{32,96},{40,8},{48,112},{56,24},{64,... | collective-permute-start | bytes 245768 | tf_op jit(solution)/shard_map/ppermute | solution.py:284
  8.1 5.0 %collective-permute-start.1 = (f32[20,8,128]{2,1,0:T(8,128)S(1)}, f32[20,8,128]{2,1,0:T(8,128)S(1)}, u32[]{:S(2)}, u32[]{:S(2)}) collective-permute-start(f32[20,8,128]{2,1,0:T(8,128)S(1)} %get-tuple-element.19.own_ref.after), channel_id=1, source_target_pairs={{0,64},{8,24},{16,80},{24,8},{32,96},{40,56},{48,112},{56,40},{64,... | collective-permute-start | bytes 245768 | tf_op jit(solution)/shard_map/ppermute | solution.py:284
  13.2 4.9 %collective-permute-start.6 = (f32[20,8,128]{2,1,0:T(8,128)S(1)}, f32[20,8,128]{2,1,0:T(8,128)S(1)}, u32[]{:S(2)}, u32[]{:S(2)}) collective-permute-start(f32[20,8,128]{2,1,0:T(8,128)S(1)} %get-tuple-element.20.own_ref), channel_id=1, source_target_pairs={{0,16},{8,200},{16,0},{24,216},{32,48},{40,232},{48,32},{56,248},{... | collective-permute-start | bytes 245768 | tf_op jit(solution)/shard_map/ppermute | solution.py:284
  15.4 4.8 %collective-permute-start.5 = (f32[20,8,128]{2,1,0:T(8,128)S(1)}, f32[20,8,128]{2,1,0:T(8,128)S(1)}, u32[]{:S(2)}, u32[]{:S(2)}) collective-permute-start(f32[20,8,128]{2,1,0:T(8,128)S(1)} %get-tuple-element.20.own_ref), channel_id=1, source_target_pairs={{0,16},{8,136},{16,0},{24,152},{32,48},{40,168},{48,32},{56,184},{... | collective-permute-start | bytes 245768 | tf_op jit(solution)/shard_map/ppermute | solution.py:284
  15.7 4.4 %collective-permute-start.4 = (f32[20,8,128]{2,1,0:T(8,128)S(1)}, f32[20,8,128]{2,1,0:T(8,128)S(1)}, u32[]{:S(2)}, u32[]{:S(2)}) collective-permute-start(f32[20,8,128]{2,1,0:T(8,128)S(1)} %get-tuple-element.20.own_ref), channel_id=1, source_target_pairs={{0,16},{8,72},{16,0},{24,88},{32,48},{40,104},{48,32},{56,120},{64... | collective-permute-start | bytes 245768 | tf_op jit(solution)/shard_map/ppermute | solution.py:284
  20.3 1.3 %collective-permute-start.7 = (f32[4,8,128]{2,1,0:T(8,128)S(1)}, f32[4,8,128]{2,1,0:T(8,128)S(1)}, u32[]{:S(2)}, u32[]{:S(2)}) collective-permute-start(f32[4,8,128]{2,1,0:T(8,128)S(1)} %get-tuple-element.29), channel_id=1, source_target_pairs={{0,8},{8,0},{16,24},{24,16},{32,40},{40,32},{48,56},{56,48},{64,72... | collective-permute-start | bytes 49160 | tf_op jit(solution)/shard_map/ppermute | solution.py:284

commit v3 on v2

--- a/solution.py
+++ b/solution.py
@@ -6,8 +6,9 @@
 from jax.sharding import PartitionSpec as P
 
 ROWS = 128
-SUBS = 4
-CHUNKS = 4
+SUBS = 2
+CHUNKS = 8
+WRITES = 4
 TILE = (8, 128)
 VMEM_BYTES = 12 << 20
 
@@ -112,6 +113,11 @@
 
 def row_of(buffers, sub, chunk, step):
     return tuple(buf[sub, chunk, pl.ds(step, 8, stride=8), :] for buf in buffers)
+
+
+def place_of(i):
+    block, step = divmod(i, 8)
+    return block // CHUNKS, block % CHUNKS, step
 
 
 def port_kernel(*refs):
@@ -164,7 +170,7 @@
     buffers = (l2, l1, u1, u2, tr)
     far, near = None, None
     for i in range(ROWS):
-        coefs = row_of(buffers, i // 32, (i // 8) % 4, i % 8)
+        coefs = row_of(buffers, *place_of(i))
         if i == 0:
             row = eliminate_first(coefs)
         elif i == 1:
@@ -182,7 +188,7 @@
         p, q = p_buf[i], q_buf[i]
         own = mix((p, q), next1, next2)
         own = (own[0] + out[0, i], own[1] + out[1, i], own[2] + out[2, i], own[3], own[4])
-        target = tr[i // 32, (i // 8) % 4, pl.ds(i % 8, 8, stride=8), :]
+        (target,) = row_of((tr,), *place_of(i))
         out[0, i] = own[0] + own[0] - target
         for k in range(1, 5):
             out[k, i] = own[k]
@@ -251,15 +257,17 @@
     is_high = lax.axis_index("lon") % 2 == 1
     weights = [jnp.where(is_high, high_own[k], received[k]) for k in range(4)]
     copies = []
-    for s in range(SUBS):
-        for c in range(CHUNKS):
+    size = ROWS // 8 // WRITES
+    for piece in range(WRITES):
+        for block in range(piece * size, (piece + 1) * size):
             for step in range(8):
-                i = 32 * s + 8 * c + step
+                i = 8 * block + step
                 value = spikes[0, i]
                 for k in range(4):
                     value = value + spikes[k + 1, i] * weights[k]
-                stage[s, c, pl.ds(step, 8, stride=8), :] = value
-        copy = pltpu.make_async_copy(stage.at[s], out.at[s], sems.at[s])
+                stage[block, pl.ds(step, 8, stride=8), :] = value
+        span = pl.ds(piece * size, size)
+        copy = pltpu.make_async_copy(stage.at[span], out.at[span], sems.at[piece])
         copy.start()
         copies.append(copy)
     for copy in copies:
@@ -288,6 +296,7 @@
     vmem = pl.BlockSpec(memory_space=pltpu.VMEM)
     hbm = pl.BlockSpec(memory_space=pltpu.HBM)
     tiles = (SUBS, CHUNKS, 64, 128)
+    blocks = (SUBS * CHUNKS, 64, 128)
 
     def view(array):
         return array.reshape(16, 8, 8, 128).transpose(0, 2, 1, 3).reshape(tiles)
@@ -326,10 +335,10 @@
     )
     (out,) = call(
         combine_kernel,
-        [tiles],
+        [blocks],
         [exchange(low_ends, 1, 1), high_ends, spikes],
         out_specs=[hbm],
-        scratch=[pltpu.VMEM(tiles, jnp.float32), pltpu.SemaphoreType.DMA((SUBS,))],
+        scratch=[pltpu.VMEM(blocks, jnp.float32), pltpu.SemaphoreType.DMA((WRITES,))],
         name="combine",
     )
     return out.reshape(16, 8, 8, 128).transpose(0, 2, 1, 3).reshape(ROWS, 1024)

time: 22.5 us -> 22.5 us (level)
  no operation moved by 1% of the time
where the time goes in v3:
time: 22.5 us; the launch traced here: 22.4 us
  starting transfers between devices  10.3 us (46%)
  waiting for transfers between devices  6.88 us (31%)
  Pallas kernels  5.12 us (23%)
    ppermute x8, starting transfers between devices, exchange(): return lax.ppermute(port, 'lon', pairs)  10.3 us
    ppermute x8, waiting for transfers between devices, exchange(): return lax.ppermute(port, 'lon', pairs)  6.88 us
    pallas_call x6, Pallas kernels, call(): pl.pallas_call(kernel, out_shape=[jax.ShapeDtypeStruct(shape, jnp.float32...  5.12 us
  transfers between devices with their start and end apart: 8, of which 6 were waited for; matrix products, arithmetic and copies ran while one was open for 0% of the time, Pallas kernels for 7%

profile of v3, /device:TPU:1, one launch (start us, length us, event | category | flops | bytes accessed | tf_op | source)
XLA Modules:
  0.0 22.4 jit_solution(14627639788858697859)
XLA Ops:
  0.0 2.4 %segment_port.1 = (f32[20,8,128]{2,1,0:T(8,128)S(1)}, f32[2,8,64,128]{3,2,1,0:T(8,128)S(1)}, f32[2,8,64,128]{3,2,1,0:T(8,128)S(1)}, f32[2,8,64,128]{3,2,1,0:T(8,...) custom-call(f32[2,8,64,128]{3,2,1,0:T(8,128)} %bitcast.30, f32[2,8,64,128]{3,2,1,0:T(8,128)} %bitcast.31, ...), custom_call_target="tpu_custom_call" | custom-call | tf_op jit(solution)/shard_map/segment_port/pallas_call | solution.py:279
  2.4 3.3 %collective-permute-start = (f32[20,8,128]{2,1,0:T(8,128)S(1)}, f32[20,8,128]{2,1,0:T(8,128)S(1)}, u32[]{:S(2)}, u32[]{:S(2)}) collective-permute-start(f32[20,8,128]{2,1,0:T(8,128)S(1)} %get-tuple-element.18.own_ref), channel_id=1, source_target_pairs={{0,8},{8,0},{16,24},{24,16},{32,40},{40,32},{48,56},{56,48},{64,72... | collective-permute-start | bytes 245768 | tf_op jit(solution)/shard_map/ppermute | solution.py:292
  5.7 0.9 %collective-permute-done.other_ref = f32[20,8,128]{2,1,0:T(8,128)S(1)} collective-permute-done((f32[20,8,128]{2,1,0:T(8,128)S(1)}, f32[20,8,128]{2,1,0:T(8,128)S(1)}, u32[]{:S(2)}, u32[]{:S(2)}) %collective-permute-start) | collective-permute-done | bytes 81952 | tf_op jit(solution)/shard_map/ppermute | solution.py:292
  6.7 0.8 %collective-permute-start.3 = (f32[20,8,128]{2,1,0:T(8,128)S(1)}, f32[20,8,128]{2,1,0:T(8,128)S(1)}, u32[]{:S(2)}, u32[]{:S(2)}) collective-permute-start(f32[20,8,128]{2,1,0:T(8,128)S(1)} %get-tuple-element.19.own_ref.after), channel_id=1, source_target_pairs={{0,64},{8,56},{16,80},{24,40},{32,96},{40,24},{48,112},{56,8},{64,... | collective-permute-start | bytes 245768 | tf_op jit(solution)/shard_map/ppermute | solution.py:292
  7.5 0.5 %collective-permute-start.2 = (f32[20,8,128]{2,1,0:T(8,128)S(1)}, f32[20,8,128]{2,1,0:T(8,128)S(1)}, u32[]{:S(2)}, u32[]{:S(2)}) collective-permute-start(f32[20,8,128]{2,1,0:T(8,128)S(1)} %get-tuple-element.19.own_ref.after), channel_id=1, source_target_pairs={{0,64},{8,40},{16,80},{24,56},{32,96},{40,8},{48,112},{56,24},{64,... | collective-permute-start | bytes 245768 | tf_op jit(solution)/shard_map/ppermute | solution.py:292
  8.0 2.0 %collective-permute-start.1 = (f32[20,8,128]{2,1,0:T(8,128)S(1)}, f32[20,8,128]{2,1,0:T(8,128)S(1)}, u32[]{:S(2)}, u32[]{:S(2)}) collective-permute-start(f32[20,8,128]{2,1,0:T(8,128)S(1)} %get-tuple-element.19.own_ref.after), channel_id=1, source_target_pairs={{0,64},{8,24},{16,80},{24,8},{32,96},{40,56},{48,112},{56,40},{64,... | collective-permute-start | bytes 245768 | tf_op jit(solution)/shard_map/ppermute | solution.py:292
  10.0 1.2 %collective-permute-done.3.by3 = f32[20,8,128]{2,1,0:T(8,128)S(1)} collective-permute-done((f32[20,8,128]{2,1,0:T(8,128)S(1)}, f32[20,8,128]{2,1,0:T(8,128)S(1)}, u32[]{:S(2)}, u32[]{:S(2)}) %collective-permute-start.3) | collective-permute-done | bytes 81952 | tf_op jit(solution)/shard_map/ppermute | solution.py:292
  11.3 1.0 %collective-permute-done.2.by2 = f32[20,8,128]{2,1,0:T(8,128)S(1)} collective-permute-done((f32[20,8,128]{2,1,0:T(8,128)S(1)}, f32[20,8,128]{2,1,0:T(8,128)S(1)}, u32[]{:S(2)}, u32[]{:S(2)}) %collective-permute-start.2) | collective-permute-done | bytes 81952 | tf_op jit(solution)/shard_map/ppermute | solution.py:292
  12.3 0.7 %collective-permute-done.1.by1 = f32[20,8,128]{2,1,0:T(8,128)S(1)} collective-permute-done((f32[20,8,128]{2,1,0:T(8,128)S(1)}, f32[20,8,128]{2,1,0:T(8,128)S(1)}, u32[]{:S(2)}, u32[]{:S(2)}) %collective-permute-start.1) | collective-permute-done | bytes 81952 | tf_op jit(solution)/shard_map/ppermute | solution.py:292
  13.0 0.1 x_join.1
  13.2 2.1 %collective-permute-start.6 = (f32[20,8,128]{2,1,0:T(8,128)S(1)}, f32[20,8,128]{2,1,0:T(8,128)S(1)}, u32[]{:S(2)}, u32[]{:S(2)}) collective-permute-start(f32[20,8,128]{2,1,0:T(8,128)S(1)} %get-tuple-element.20.own_ref), channel_id=1, source_target_pairs={{0,16},{8,200},{16,0},{24,216},{32,48},{40,232},{48,32},{56,248},{... | collective-permute-start | bytes 245768 | tf_op jit(solution)/shard_map/ppermute | solution.py:292
  15.3 0.3 %collective-permute-start.5 = (f32[20,8,128]{2,1,0:T(8,128)S(1)}, f32[20,8,128]{2,1,0:T(8,128)S(1)}, u32[]{:S(2)}, u32[]{:S(2)}) collective-permute-start(f32[20,8,128]{2,1,0:T(8,128)S(1)} %get-tuple-element.20.own_ref), channel_id=1, source_target_pairs={{0,16},{8,136},{16,0},{24,152},{32,48},{40,168},{48,32},{56,184},{... | collective-permute-start | bytes 245768 | tf_op jit(solution)/shard_map/ppermute | solution.py:292
  15.6 0.9 %collective-permute-start.4 = (f32[20,8,128]{2,1,0:T(8,128)S(1)}, f32[20,8,128]{2,1,0:T(8,128)S(1)}, u32[]{:S(2)}, u32[]{:S(2)}) collective-permute-start(f32[20,8,128]{2,1,0:T(8,128)S(1)} %get-tuple-element.20.own_ref), channel_id=1, source_target_pairs={{0,16},{8,72},{16,0},{24,88},{32,48},{40,104},{48,32},{56,120},{64... | collective-permute-start | bytes 245768 | tf_op jit(solution)/shard_map/ppermute | solution.py:292
  16.5 1.6 %segment_spikes.1.before.spikes = f32[5,128,8,128]{3,2,1,0:T(8,128)S(1)} custom-call(f32[2,8,64,128]{3,2,1,0:T(8,128)S(1)} %get-tuple-element.24.l2, f32[2,8,64,128]{3,2,1,0:T(8,128)S(1)} %get-tuple-element.25.l1, f32[2,8,64,128]{3,2,1,0:T(8,128)S(1)} %get-tuple-element.26.u1, f32[2,8,64,128]{3,2,1,0:T(8,128)S(1)} %get-tuple-element.27.u2, ...), custom_call_target="tpu_custom_call" | custom-call | tf_op jit(solution)/shard_map/segment_spikes/pallas_call | solution.py:279
  18.1 0.0 collective-permute-done.6.by3
  18.1 2.0 %collective-permute-done.5.by2 = f32[20,8,128]{2,1,0:T(8,128)S(1)} collective-permute-done((f32[20,8,128]{2,1,0:T(8,128)S(1)}, f32[20,8,128]{2,1,0:T(8,128)S(1)}, u32[]{:S(2)}, u32[]{:S(2)}) %collective-permute-start.5) | collective-permute-done | bytes 81952 | tf_op jit(solution)/shard_map/ppermute | solution.py:292
  20.1 0.0 collective-permute-done.4.by1
  20.1 0.1 y_solve.1
  20.2 0.3 %collective-permute-start.7 = (f32[4,8,128]{2,1,0:T(8,128)S(1)}, f32[4,8,128]{2,1,0:T(8,128)S(1)}, u32[]{:S(2)}, u32[]{:S(2)}) collective-permute-start(f32[4,8,128]{2,1,0:T(8,128)S(1)} %get-tuple-element.29), channel_id=1, source_target_pairs={{0,8},{8,0},{16,24},{24,16},{32,40},{40,32},{48,56},{56,48},{64,72... | collective-permute-start | bytes 49160 | tf_op jit(solution)/shard_map/ppermute | solution.py:292
  20.5 1.0 %collective-permute-done.7.received = f32[4,8,128]{2,1,0:T(8,128)S(1)} collective-permute-done((f32[4,8,128]{2,1,0:T(8,128)S(1)}, f32[4,8,128]{2,1,0:T(8,128)S(1)}, u32[]{:S(2)}, u32[]{:S(2)}) %collective-permute-start.7) | collective-permute-done | bytes 16416 | tf_op jit(solution)/shard_map/ppermute | solution.py:292
  21.5 0.9 %combine.1 = f32[16,64,128]{2,1,0:T(8,128)} custom-call(f32[4,8,128]{2,1,0:T(8,128)S(1)} %collective-permute-done.7.received, f32[4,8,128]{2,1,0:T(8,128)S(1)} %get-tuple-element.30.high_own, f32[5,128,8,128]{3,2,1,0:T(8,128)S(1)} %segment_spikes.1.before.spikes), custom_call_target="tpu_custom_call" | custom-call | tf_op jit(solution)/shard_map/combine/pallas_call | solution.py:279
  (1 shorter events, 0.0 us)
Async XLA Ops:
  2.4 4.3 %collective-permute-start = (f32[20,8,128]{2,1,0:T(8,128)S(1)}, f32[20,8,128]{2,1,0:T(8,128)S(1)}, u32[]{:S(2)}, u32[]{:S(2)}) collective-permute-start(f32[20,8,128]{2,1,0:T(8,128)S(1)} %get-tuple-element.18.own_ref), channel_id=1, source_target_pairs={{0,8},{8,0},{16,24},{24,16},{32,40},{40,32},{48,56},{56,48},{64,72... | collective-permute-start | bytes 245768 | tf_op jit(solution)/shard_map/ppermute | solution.py:292
  6.7 4.6 %collective-permute-start.3 = (f32[20,8,128]{2,1,0:T(8,128)S(1)}, f32[20,8,128]{2,1,0:T(8,128)S(1)}, u32[]{:S(2)}, u32[]{:S(2)}) collective-permute-start(f32[20,8,128]{2,1,0:T(8,128)S(1)} %get-tuple-element.19.own_ref.after), channel_id=1, source_target_pairs={{0,64},{8,56},{16,80},{24,40},{32,96},{40,24},{48,112},{56,8},{64,... | collective-permute-start | bytes 245768 | tf_op jit(solution)/shard_map/ppermute | solution.py:292
  7.5 4.8 %collective-permute-start.2 = (f32[20,8,128]{2,1,0:T(8,128)S(1)}, f32[20,8,128]{2,1,0:T(8,128)S(1)}, u32[]{:S(2)}, u32[]{:S(2)}) collective-permute-start(f32[20,8,128]{2,1,0:T(8,128)S(1)} %get-tuple-element.19.own_ref.after), channel_id=1, source_target_pairs={{0,64},{8,40},{16,80},{24,56},{32,96},{40,8},{48,112},{56,24},{64,... | collective-permute-start | bytes 245768 | tf_op jit(solution)/shard_map/ppermute | solution.py:292
  8.0 5.0 %collective-permute-start.1 = (f32[20,8,128]{2,1,0:T(8,128)S(1)}, f32[20,8,128]{2,1,0:T(8,128)S(1)}, u32[]{:S(2)}, u32[]{:S(2)}) collective-permute-start(f32[20,8,128]{2,1,0:T(8,128)S(1)} %get-tuple-element.19.own_ref.after), channel_id=1, source_target_pairs={{0,64},{8,24},{16,80},{24,8},{32,96},{40,56},{48,112},{56,40},{64,... | collective-permute-start | bytes 245768 | tf_op jit(solution)/shard_map/ppermute | solution.py:292
  13.2 4.9 %collective-permute-start.6 = (f32[20,8,128]{2,1,0:T(8,128)S(1)}, f32[20,8,128]{2,1,0:T(8,128)S(1)}, u32[]{:S(2)}, u32[]{:S(2)}) collective-permute-start(f32[20,8,128]{2,1,0:T(8,128)S(1)} %get-tuple-element.20.own_ref), channel_id=1, source_target_pairs={{0,16},{8,200},{16,0},{24,216},{32,48},{40,232},{48,32},{56,248},{... | collective-permute-start | bytes 245768 | tf_op jit(solution)/shard_map/ppermute | solution.py:292
  15.3 4.8 %collective-permute-start.5 = (f32[20,8,128]{2,1,0:T(8,128)S(1)}, f32[20,8,128]{2,1,0:T(8,128)S(1)}, u32[]{:S(2)}, u32[]{:S(2)}) collective-permute-start(f32[20,8,128]{2,1,0:T(8,128)S(1)} %get-tuple-element.20.own_ref), channel_id=1, source_target_pairs={{0,16},{8,136},{16,0},{24,152},{32,48},{40,168},{48,32},{56,184},{... | collective-permute-start | bytes 245768 | tf_op jit(solution)/shard_map/ppermute | solution.py:292
  15.6 4.4 %collective-permute-start.4 = (f32[20,8,128]{2,1,0:T(8,128)S(1)}, f32[20,8,128]{2,1,0:T(8,128)S(1)}, u32[]{:S(2)}, u32[]{:S(2)}) collective-permute-start(f32[20,8,128]{2,1,0:T(8,128)S(1)} %get-tuple-element.20.own_ref), channel_id=1, source_target_pairs={{0,16},{8,72},{16,0},{24,88},{32,48},{40,104},{48,32},{56,120},{64... | collective-permute-start | bytes 245768 | tf_op jit(solution)/shard_map/ppermute | solution.py:292
  20.2 1.3 %collective-permute-start.7 = (f32[4,8,128]{2,1,0:T(8,128)S(1)}, f32[4,8,128]{2,1,0:T(8,128)S(1)}, u32[]{:S(2)}, u32[]{:S(2)}) collective-permute-start(f32[4,8,128]{2,1,0:T(8,128)S(1)} %get-tuple-element.29), channel_id=1, source_target_pairs={{0,8},{8,0},{16,24},{24,16},{32,40},{40,32},{48,56},{56,48},{64,72... | collective-permute-start | bytes 49160 | tf_op jit(solution)/shard_map/ppermute | solution.py:292

commit v4 on v3

--- a/solution.py
+++ b/solution.py
@@ -253,9 +253,8 @@
         high_out[k] = value + value
 
 
-def combine_kernel(received, high_own, spikes, out, stage, sems):
-    is_high = lax.axis_index("lon") % 2 == 1
-    weights = [jnp.where(is_high, high_own[k], received[k]) for k in range(4)]
+def combine(ends, spikes, out, stage, sems):
+    weights = [ends[k] for k in range(4)]
     copies = []
     size = ROWS // 8 // WRITES
     for piece in range(WRITES):
@@ -274,7 +273,21 @@
         copy.wait()
 
 
-def call(kernel, outs, operands, out_specs=None, in_specs=None, scratch=(), name=None):
+def combine_odd_kernel(ends, spikes, out, stage, sems):
+    @pl.when(lax.axis_index("lon") % 2 == 1)
+    def _():
+        combine(ends, spikes, out, stage, sems)
+
+
+def combine_even_kernel(ends, spikes, partial, out, stage, sems):
+    @pl.when(lax.axis_index("lon") % 2 == 0)
+    def _():
+        combine(ends, spikes, out, stage, sems)
+
+
+def call(
+    kernel, outs, operands, out_specs=None, in_specs=None, scratch=(), name=None, aliases={}
+):
     vmem = pl.BlockSpec(memory_space=pltpu.VMEM)
     return pl.pallas_call(
         kernel,
@@ -283,6 +296,7 @@
         out_specs=out_specs or [vmem] * len(outs),
         scratch_shapes=list(scratch),
         compiler_params=pltpu.CompilerParams(vmem_limit_bytes=VMEM_BYTES),
+        input_output_aliases=aliases,
         name=name,
     )(*operands)
 
@@ -333,13 +347,25 @@
         [group] + by_y + [top_x, pair_x, core_split, spikes],
         name="y_solve",
     )
+    received = exchange(low_ends, 1, 1)
+    scratch = [pltpu.VMEM(blocks, jnp.float32), pltpu.SemaphoreType.DMA((WRITES,))]
     (out,) = call(
-        combine_kernel,
+        combine_odd_kernel,
         [blocks],
-        [exchange(low_ends, 1, 1), high_ends, spikes],
+        [high_ends, spikes],
         out_specs=[hbm],
-        scratch=[pltpu.VMEM(blocks, jnp.float32), pltpu.SemaphoreType.DMA((WRITES,))],
-        name="combine",
+        scratch=scratch,
+        name="combine_odd",
+    )
+    (out,) = call(
+        combine_even_kernel,
+        [blocks],
+        [received, spikes, out],
+        in_specs=[vmem, vmem, hbm],
+        out_specs=[hbm],
+        scratch=scratch,
+        name="combine_even",
+        aliases={2: 0},
     )
     return out.reshape(16, 8, 8, 128).transpose(0, 2, 1, 3).reshape(ROWS, 1024)
 

time: 22.5 us -> 21.7 us (0.964)
  waiting for transfers between devices: 6.88 us -> 6.01 us
    ppermute x8, waiting for transfers between devices: 6.88 us -> 6.01 us  [exchange(): return lax.ppermute(port, 'lon', pairs)]
    pallas_call x6 -> x7, Pallas kernels: 5.12 us -> 5.15 us  [call(): pl.pallas_call(kernel, out_shape=[jax.ShapeDtypeStruct(shape, jnp.float32...]
  transfers between devices with their start and end apart: 8 -> 8, of which waited for: 6 -> 6; matrix products, arithmetic and copies ran while one was open for 0% -> 0% of each run, Pallas kernels for 7% -> 11%
where the time goes in v4:
time: 21.7 us; the launch traced here: 21.5 us
  starting transfers between devices  10.3 us (47%)
  waiting for transfers between devices  6.01 us (28%)
  Pallas kernels  5.15 us (24%)
    ppermute x8, starting transfers between devices, exchange(): return lax.ppermute(port, 'lon', pairs)  10.3 us
    ppermute x8, waiting for transfers between devices, exchange(): return lax.ppermute(port, 'lon', pairs)  6.01 us
    pallas_call x7, Pallas kernels, call(): pl.pallas_call(kernel, out_shape=[jax.ShapeDtypeStruct(shape, jnp.float32...  5.15 us
  transfers between devices with their start and end apart: 8, of which 6 were waited for; matrix products, arithmetic and copies ran while one was open for 0% of the time, Pallas kernels for 11%

profile of v4, /device:TPU:1, one launch (start us, length us, event | category | flops | bytes accessed | tf_op | source)
XLA Modules:
  0.0 21.5 jit_solution(17331303952383900638)
XLA Ops:
  0.0 2.4 %segment_port.1 = (f32[20,8,128]{2,1,0:T(8,128)S(1)}, f32[2,8,64,128]{3,2,1,0:T(8,128)S(1)}, f32[2,8,64,128]{3,2,1,0:T(8,128)S(1)}, f32[2,8,64,128]{3,2,1,0:T(8,...) custom-call(f32[2,8,64,128]{3,2,1,0:T(8,128)} %bitcast.30, f32[2,8,64,128]{3,2,1,0:T(8,128)} %bitcast.31, ...), custom_call_target="tpu_custom_call" | custom-call | tf_op jit(solution)/shard_map/segment_port/pallas_call | solution.py:292
  2.4 3.3 %collective-permute-start = (f32[20,8,128]{2,1,0:T(8,128)S(1)}, f32[20,8,128]{2,1,0:T(8,128)S(1)}, u32[]{:S(2)}, u32[]{:S(2)}) collective-permute-start(f32[20,8,128]{2,1,0:T(8,128)S(1)} %get-tuple-element.18.own_ref), channel_id=1, source_target_pairs={{0,8},{8,0},{16,24},{24,16},{32,40},{40,32},{48,56},{56,48},{64,72... | collective-permute-start | bytes 245768 | tf_op jit(solution)/shard_map/ppermute | solution.py:306
  5.7 0.9 %collective-permute-done.other_ref = f32[20,8,128]{2,1,0:T(8,128)S(1)} collective-permute-done((f32[20,8,128]{2,1,0:T(8,128)S(1)}, f32[20,8,128]{2,1,0:T(8,128)S(1)}, u32[]{:S(2)}, u32[]{:S(2)}) %collective-permute-start) | collective-permute-done | bytes 81952 | tf_op jit(solution)/shard_map/ppermute | solution.py:306
  6.7 0.8 %collective-permute-start.3 = (f32[20,8,128]{2,1,0:T(8,128)S(1)}, f32[20,8,128]{2,1,0:T(8,128)S(1)}, u32[]{:S(2)}, u32[]{:S(2)}) collective-permute-start(f32[20,8,128]{2,1,0:T(8,128)S(1)} %get-tuple-element.19.own_ref.after), channel_id=1, source_target_pairs={{0,64},{8,56},{16,80},{24,40},{32,96},{40,24},{48,112},{56,8},{64,... | collective-permute-start | bytes 245768 | tf_op jit(solution)/shard_map/ppermute | solution.py:306
  7.5 0.5 %collective-permute-start.2 = (f32[20,8,128]{2,1,0:T(8,128)S(1)}, f32[20,8,128]{2,1,0:T(8,128)S(1)}, u32[]{:S(2)}, u32[]{:S(2)}) collective-permute-start(f32[20,8,128]{2,1,0:T(8,128)S(1)} %get-tuple-element.19.own_ref.after), channel_id=1, source_target_pairs={{0,64},{8,40},{16,80},{24,56},{32,96},{40,8},{48,112},{56,24},{64,... | collective-permute-start | bytes 245768 | tf_op jit(solution)/shard_map/ppermute | solution.py:306
  8.0 2.0 %collective-permute-start.1 = (f32[20,8,128]{2,1,0:T(8,128)S(1)}, f32[20,8,128]{2,1,0:T(8,128)S(1)}, u32[]{:S(2)}, u32[]{:S(2)}) collective-permute-start(f32[20,8,128]{2,1,0:T(8,128)S(1)} %get-tuple-element.19.own_ref.after), channel_id=1, source_target_pairs={{0,64},{8,24},{16,80},{24,8},{32,96},{40,56},{48,112},{56,40},{64,... | collective-permute-start | bytes 245768 | tf_op jit(solution)/shard_map/ppermute | solution.py:306
  10.0 1.2 %collective-permute-done.3.by3 = f32[20,8,128]{2,1,0:T(8,128)S(1)} collective-permute-done((f32[20,8,128]{2,1,0:T(8,128)S(1)}, f32[20,8,128]{2,1,0:T(8,128)S(1)}, u32[]{:S(2)}, u32[]{:S(2)}) %collective-permute-start.3) | collective-permute-done | bytes 81952 | tf_op jit(solution)/shard_map/ppermute | solution.py:306
  11.3 1.0 %collective-permute-done.2.by2 = f32[20,8,128]{2,1,0:T(8,128)S(1)} collective-permute-done((f32[20,8,128]{2,1,0:T(8,128)S(1)}, f32[20,8,128]{2,1,0:T(8,128)S(1)}, u32[]{:S(2)}, u32[]{:S(2)}) %collective-permute-start.2) | collective-permute-done | bytes 81952 | tf_op jit(solution)/shard_map/ppermute | solution.py:306
  12.3 0.7 %collective-permute-done.1.by1 = f32[20,8,128]{2,1,0:T(8,128)S(1)} collective-permute-done((f32[20,8,128]{2,1,0:T(8,128)S(1)}, f32[20,8,128]{2,1,0:T(8,128)S(1)}, u32[]{:S(2)}, u32[]{:S(2)}) %collective-permute-start.1) | collective-permute-done | bytes 81952 | tf_op jit(solution)/shard_map/ppermute | solution.py:306
  13.0 0.1 x_join.1
  13.2 2.1 %collective-permute-start.6 = (f32[20,8,128]{2,1,0:T(8,128)S(1)}, f32[20,8,128]{2,1,0:T(8,128)S(1)}, u32[]{:S(2)}, u32[]{:S(2)}) collective-permute-start(f32[20,8,128]{2,1,0:T(8,128)S(1)} %get-tuple-element.20.own_ref), channel_id=1, source_target_pairs={{0,16},{8,200},{16,0},{24,216},{32,48},{40,232},{48,32},{56,248},{... | collective-permute-start | bytes 245768 | tf_op jit(solution)/shard_map/ppermute | solution.py:306
  15.3 0.3 %collective-permute-start.5 = (f32[20,8,128]{2,1,0:T(8,128)S(1)}, f32[20,8,128]{2,1,0:T(8,128)S(1)}, u32[]{:S(2)}, u32[]{:S(2)}) collective-permute-start(f32[20,8,128]{2,1,0:T(8,128)S(1)} %get-tuple-element.20.own_ref), channel_id=1, source_target_pairs={{0,16},{8,136},{16,0},{24,152},{32,48},{40,168},{48,32},{56,184},{... | collective-permute-start | bytes 245768 | tf_op jit(solution)/shard_map/ppermute | solution.py:306
  15.6 0.9 %collective-permute-start.4 = (f32[20,8,128]{2,1,0:T(8,128)S(1)}, f32[20,8,128]{2,1,0:T(8,128)S(1)}, u32[]{:S(2)}, u32[]{:S(2)}) collective-permute-start(f32[20,8,128]{2,1,0:T(8,128)S(1)} %get-tuple-element.20.own_ref), channel_id=1, source_target_pairs={{0,16},{8,72},{16,0},{24,88},{32,48},{40,104},{48,32},{56,120},{64... | collective-permute-start | bytes 245768 | tf_op jit(solution)/shard_map/ppermute | solution.py:306
  16.5 1.6 %segment_spikes.1.before.spikes = f32[5,128,8,128]{3,2,1,0:T(8,128)S(1)} custom-call(f32[2,8,64,128]{3,2,1,0:T(8,128)S(1)} %get-tuple-element.24.l2, f32[2,8,64,128]{3,2,1,0:T(8,128)S(1)} %get-tuple-element.25.l1, f32[2,8,64,128]{3,2,1,0:T(8,128)S(1)} %get-tuple-element.26.u1, f32[2,8,64,128]{3,2,1,0:T(8,128)S(1)} %get-tuple-element.27.u2, ...), custom_call_target="tpu_custom_call" | custom-call | tf_op jit(solution)/shard_map/segment_spikes/pallas_call | solution.py:292
  18.1 0.0 collective-permute-done.6.by3
  18.1 2.0 %collective-permute-done.5.by2 = f32[20,8,128]{2,1,0:T(8,128)S(1)} collective-permute-done((f32[20,8,128]{2,1,0:T(8,128)S(1)}, f32[20,8,128]{2,1,0:T(8,128)S(1)}, u32[]{:S(2)}, u32[]{:S(2)}) %collective-permute-start.5) | collective-permute-done | bytes 81952 | tf_op jit(solution)/shard_map/ppermute | solution.py:306
  20.1 0.0 collective-permute-done.4.by1
  20.1 0.1 y_solve.1
  20.2 0.3 %collective-permute-start.7 = (f32[4,8,128]{2,1,0:T(8,128)S(1)}, f32[4,8,128]{2,1,0:T(8,128)S(1)}, u32[]{:S(2)}, u32[]{:S(2)}) collective-permute-start(f32[4,8,128]{2,1,0:T(8,128)S(1)} %get-tuple-element.29), channel_id=1, source_target_pairs={{0,8},{8,0},{16,24},{24,16},{32,40},{40,32},{48,56},{56,48},{64,72... | collective-permute-start | bytes 49160 | tf_op jit(solution)/shard_map/ppermute | solution.py:306
  20.5 0.9 %combine_odd.1.partial = f32[16,64,128]{2,1,0:T(8,128)} custom-call(f32[4,8,128]{2,1,0:T(8,128)S(1)} %get-tuple-element.30.ends, f32[5,128,8,128]{3,2,1,0:T(8,128)S(1)} %segment_spikes.1.before.spikes), custom_call_target="tpu_custom_call" | custom-call | tf_op jit(solution)/shard_map/combine_odd/pallas_call | solution.py:292
  21.4 0.1 collective-permute-done.7.ends
  (2 shorter events, 0.1 us)
Async XLA Ops:
  2.4 4.3 %collective-permute-start = (f32[20,8,128]{2,1,0:T(8,128)S(1)}, f32[20,8,128]{2,1,0:T(8,128)S(1)}, u32[]{:S(2)}, u32[]{:S(2)}) collective-permute-start(f32[20,8,128]{2,1,0:T(8,128)S(1)} %get-tuple-element.18.own_ref), channel_id=1, source_target_pairs={{0,8},{8,0},{16,24},{24,16},{32,40},{40,32},{48,56},{56,48},{64,72... | collective-permute-start | bytes 245768 | tf_op jit(solution)/shard_map/ppermute | solution.py:306
  6.7 4.6 %collective-permute-start.3 = (f32[20,8,128]{2,1,0:T(8,128)S(1)}, f32[20,8,128]{2,1,0:T(8,128)S(1)}, u32[]{:S(2)}, u32[]{:S(2)}) collective-permute-start(f32[20,8,128]{2,1,0:T(8,128)S(1)} %get-tuple-element.19.own_ref.after), channel_id=1, source_target_pairs={{0,64},{8,56},{16,80},{24,40},{32,96},{40,24},{48,112},{56,8},{64,... | collective-permute-start | bytes 245768 | tf_op jit(solution)/shard_map/ppermute | solution.py:306
  7.5 4.8 %collective-permute-start.2 = (f32[20,8,128]{2,1,0:T(8,128)S(1)}, f32[20,8,128]{2,1,0:T(8,128)S(1)}, u32[]{:S(2)}, u32[]{:S(2)}) collective-permute-start(f32[20,8,128]{2,1,0:T(8,128)S(1)} %get-tuple-element.19.own_ref.after), channel_id=1, source_target_pairs={{0,64},{8,40},{16,80},{24,56},{32,96},{40,8},{48,112},{56,24},{64,... | collective-permute-start | bytes 245768 | tf_op jit(solution)/shard_map/ppermute | solution.py:306
  8.0 5.0 %collective-permute-start.1 = (f32[20,8,128]{2,1,0:T(8,128)S(1)}, f32[20,8,128]{2,1,0:T(8,128)S(1)}, u32[]{:S(2)}, u32[]{:S(2)}) collective-permute-start(f32[20,8,128]{2,1,0:T(8,128)S(1)} %get-tuple-element.19.own_ref.after), channel_id=1, source_target_pairs={{0,64},{8,24},{16,80},{24,8},{32,96},{40,56},{48,112},{56,40},{64,... | collective-permute-start | bytes 245768 | tf_op jit(solution)/shard_map/ppermute | solution.py:306
  13.2 4.9 %collective-permute-start.6 = (f32[20,8,128]{2,1,0:T(8,128)S(1)}, f32[20,8,128]{2,1,0:T(8,128)S(1)}, u32[]{:S(2)}, u32[]{:S(2)}) collective-permute-start(f32[20,8,128]{2,1,0:T(8,128)S(1)} %get-tuple-element.20.own_ref), channel_id=1, source_target_pairs={{0,16},{8,200},{16,0},{24,216},{32,48},{40,232},{48,32},{56,248},{... | collective-permute-start | bytes 245768 | tf_op jit(solution)/shard_map/ppermute | solution.py:306
  15.3 4.8 %collective-permute-start.5 = (f32[20,8,128]{2,1,0:T(8,128)S(1)}, f32[20,8,128]{2,1,0:T(8,128)S(1)}, u32[]{:S(2)}, u32[]{:S(2)}) collective-permute-start(f32[20,8,128]{2,1,0:T(8,128)S(1)} %get-tuple-element.20.own_ref), channel_id=1, source_target_pairs={{0,16},{8,136},{16,0},{24,152},{32,48},{40,168},{48,32},{56,184},{... | collective-permute-start | bytes 245768 | tf_op jit(solution)/shard_map/ppermute | solution.py:306
  15.6 4.4 %collective-permute-start.4 = (f32[20,8,128]{2,1,0:T(8,128)S(1)}, f32[20,8,128]{2,1,0:T(8,128)S(1)}, u32[]{:S(2)}, u32[]{:S(2)}) collective-permute-start(f32[20,8,128]{2,1,0:T(8,128)S(1)} %get-tuple-element.20.own_ref), channel_id=1, source_target_pairs={{0,16},{8,72},{16,0},{24,88},{32,48},{40,104},{48,32},{56,120},{64... | collective-permute-start | bytes 245768 | tf_op jit(solution)/shard_map/ppermute | solution.py:306
  20.2 1.3 %collective-permute-start.7 = (f32[4,8,128]{2,1,0:T(8,128)S(1)}, f32[4,8,128]{2,1,0:T(8,128)S(1)}, u32[]{:S(2)}, u32[]{:S(2)}) collective-permute-start(f32[4,8,128]{2,1,0:T(8,128)S(1)} %get-tuple-element.29), channel_id=1, source_target_pairs={{0,8},{8,0},{16,24},{24,16},{32,40},{40,32},{48,56},{56,48},{64,72... | collective-permute-start | bytes 49160 | tf_op jit(solution)/shard_map/ppermute | solution.py:306

commit v5 on v4

--- a/solution.py
+++ b/solution.py
@@ -8,7 +8,7 @@
 ROWS = 128
 SUBS = 2
 CHUNKS = 8
-WRITES = 4
+WRITES = 8
 TILE = (8, 128)
 VMEM_BYTES = 12 << 20
 
@@ -209,7 +209,7 @@
     return place % 2 == 1, place // 2 == 1
 
 
-def group_kernel(own_ref, by1, by2, by3, out, split_pair, split_top):
+def group_kernel(own_ref, by1, by3, by2, out, split_pair, split_top):
     low_bit, high_bit = bits(2)
     first, second = swap_if(low_bit, read_port(own_ref), read_port(by1))
     split = split_of(first, second)
@@ -231,7 +231,7 @@
     return new_w, new_e
 
 
-def solve_kernel(own_ref, by1, by2, by3, top_x, pair_x, core, before, low_out, high_out):
+def solve_kernel(own_ref, by1, by3, by2, top_x, pair_x, core, before, low_out, high_out):
     low_bit, high_bit = bits(8)
     first, second = swap_if(low_bit, read_port(own_ref), read_port(by1))
     split_mine = split_of(first, second)
@@ -331,7 +331,7 @@
     chip, core_split = call(
         core_kernel, [port_shape] * 2, [port, exchange(port, 1, 1)], name="core_join"
     )
-    by_x = [exchange(chip, k, 8) for k in (2, 4, 6)]
+    x_near, x_end, x_far = (exchange(chip, k, 8) for k in (2, 6, 4))
     (spikes,) = call(
         spikes_kernel,
         [(5, ROWS) + TILE],
@@ -339,12 +339,12 @@
         scratch=[pltpu.VMEM((ROWS,) + TILE, jnp.float32)] * 2,
         name="segment_spikes",
     )
-    group, pair_x, top_x = call(group_kernel, [port_shape] * 3, [chip] + by_x, name="x_join")
-    by_y = [exchange(group, k, 2) for k in (8, 16, 24)]
+    group, pair_x, top_x = call(group_kernel, [port_shape] * 3, [chip, x_near, x_end, x_far], name="x_join")
+    y_near, y_end, y_far = (exchange(group, k, 2) for k in (8, 24, 16))
     low_ends, high_ends = call(
         solve_kernel,
         [(4,) + TILE] * 2,
-        [group] + by_y + [top_x, pair_x, core_split, spikes],
+        [group, y_near, y_end, y_far, top_x, pair_x, core_split, spikes],
         name="y_solve",
     )
     received = exchange(low_ends, 1, 1)

time: 21.7 us -> 21.6 us (level)
  transfers between devices with their start and end apart: 8 -> 8, of which waited for: 6 -> 4; matrix products, arithmetic and copies ran while one was open for 0% -> 0% of each run, Pallas kernels for 11% -> 11%
where the time goes in v5:
time: 21.6 us; the launch traced here: 21.5 us
  starting transfers between devices  10.1 us (47%)
  waiting for transfers between devices  6.1 us (28%)
  Pallas kernels  5.22 us (24%)
    ppermute x8, starting transfers between devices, exchange(): return lax.ppermute(port, 'lon', pairs)  10.1 us
    ppermute x8, waiting for transfers between devices, exchange(): return lax.ppermute(port, 'lon', pairs)  6.1 us
    pallas_call x7, Pallas kernels, call(): pl.pallas_call(kernel, out_shape=[jax.ShapeDtypeStruct(shape, jnp.float32...  5.22 us
  transfers between devices with their start and end apart: 8, of which 4 were waited for; matrix products, arithmetic and copies ran while one was open for 0% of the time, Pallas kernels for 11%

profile of v5, /device:TPU:1, one launch (start us, length us, event | category | flops | bytes accessed | tf_op | source)
XLA Modules:
  0.0 21.5 jit_solution(340858750063407529)
XLA Ops:
  0.0 2.4 %segment_port.1 = (f32[20,8,128]{2,1,0:T(8,128)S(1)}, f32[2,8,64,128]{3,2,1,0:T(8,128)S(1)}, f32[2,8,64,128]{3,2,1,0:T(8,128)S(1)}, f32[2,8,64,128]{3,2,1,0:T(8,...) custom-call(f32[2,8,64,128]{3,2,1,0:T(8,128)} %bitcast.30, f32[2,8,64,128]{3,2,1,0:T(8,128)} %bitcast.31, ...), custom_call_target="tpu_custom_call" | custom-call | tf_op jit(solution)/shard_map/segment_port/pallas_call | solution.py:292
  2.4 3.3 %collective-permute-start = (f32[20,8,128]{2,1,0:T(8,128)S(1)}, f32[20,8,128]{2,1,0:T(8,128)S(1)}, u32[]{:S(2)}, u32[]{:S(2)}) collective-permute-start(f32[20,8,128]{2,1,0:T(8,128)S(1)} %get-tuple-element.18.own_ref), channel_id=1, source_target_pairs={{0,8},{8,0},{16,24},{24,16},{32,40},{40,32},{48,56},{56,48},{64,72... | collective-permute-start | bytes 245768 | tf_op jit(solution)/shard_map/ppermute | solution.py:306
  5.7 0.9 %collective-permute-done.other_ref = f32[20,8,128]{2,1,0:T(8,128)S(1)} collective-permute-done((f32[20,8,128]{2,1,0:T(8,128)S(1)}, f32[20,8,128]{2,1,0:T(8,128)S(1)}, u32[]{:S(2)}, u32[]{:S(2)}) %collective-permute-start) | collective-permute-done | bytes 81952 | tf_op jit(solution)/shard_map/ppermute | solution.py:306
  6.7 1.1 %collective-permute-start.3 = (f32[20,8,128]{2,1,0:T(8,128)S(1)}, f32[20,8,128]{2,1,0:T(8,128)S(1)}, u32[]{:S(2)}, u32[]{:S(2)}) collective-permute-start(f32[20,8,128]{2,1,0:T(8,128)S(1)} %get-tuple-element.19.own_ref.after), channel_id=1, source_target_pairs={{0,64},{8,40},{16,80},{24,56},{32,96},{40,8},{48,112},{56,24},{64,... | collective-permute-start | bytes 245768 | tf_op jit(solution)/shard_map/ppermute | solution.py:306
  7.8 0.9 %collective-permute-start.2 = (f32[20,8,128]{2,1,0:T(8,128)S(1)}, f32[20,8,128]{2,1,0:T(8,128)S(1)}, u32[]{:S(2)}, u32[]{:S(2)}) collective-permute-start(f32[20,8,128]{2,1,0:T(8,128)S(1)} %get-tuple-element.19.own_ref.after), channel_id=1, source_target_pairs={{0,64},{8,56},{16,80},{24,40},{32,96},{40,24},{48,112},{56,8},{64,... | collective-permute-start | bytes 245768 | tf_op jit(solution)/shard_map/ppermute | solution.py:306
  8.6 0.8 %collective-permute-start.1 = (f32[20,8,128]{2,1,0:T(8,128)S(1)}, f32[20,8,128]{2,1,0:T(8,128)S(1)}, u32[]{:S(2)}, u32[]{:S(2)}) collective-permute-start(f32[20,8,128]{2,1,0:T(8,128)S(1)} %get-tuple-element.19.own_ref.after), channel_id=1, source_target_pairs={{0,64},{8,24},{16,80},{24,8},{32,96},{40,56},{48,112},{56,40},{64,... | collective-permute-start | bytes 245768 | tf_op jit(solution)/shard_map/ppermute | solution.py:306
  9.4 2.2 %collective-permute-done.3.by2 = f32[20,8,128]{2,1,0:T(8,128)S(1)} collective-permute-done((f32[20,8,128]{2,1,0:T(8,128)S(1)}, f32[20,8,128]{2,1,0:T(8,128)S(1)}, u32[]{:S(2)}, u32[]{:S(2)}) %collective-permute-start.3) | collective-permute-done | bytes 81952 | tf_op jit(solution)/shard_map/ppermute | solution.py:306
  11.6 0.9 %collective-permute-done.2.by3 = f32[20,8,128]{2,1,0:T(8,128)S(1)} collective-permute-done((f32[20,8,128]{2,1,0:T(8,128)S(1)}, f32[20,8,128]{2,1,0:T(8,128)S(1)}, u32[]{:S(2)}, u32[]{:S(2)}) %collective-permute-start.2) | collective-permute-done | bytes 81952 | tf_op jit(solution)/shard_map/ppermute | solution.py:306
  12.5 0.0 collective-permute-done.1.by1
  12.5 0.1 x_join.1
  12.6 2.8 %collective-permute-start.6 = (f32[20,8,128]{2,1,0:T(8,128)S(1)}, f32[20,8,128]{2,1,0:T(8,128)S(1)}, u32[]{:S(2)}, u32[]{:S(2)}) collective-permute-start(f32[20,8,128]{2,1,0:T(8,128)S(1)} %get-tuple-element.20.own_ref), channel_id=1, source_target_pairs={{0,16},{8,136},{16,0},{24,152},{32,48},{40,168},{48,32},{56,184},{... | collective-permute-start | bytes 245768 | tf_op jit(solution)/shard_map/ppermute | solution.py:306
  15.4 0.8 %collective-permute-start.5 = (f32[20,8,128]{2,1,0:T(8,128)S(1)}, f32[20,8,128]{2,1,0:T(8,128)S(1)}, u32[]{:S(2)}, u32[]{:S(2)}) collective-permute-start(f32[20,8,128]{2,1,0:T(8,128)S(1)} %get-tuple-element.20.own_ref), channel_id=1, source_target_pairs={{0,16},{8,200},{16,0},{24,216},{32,48},{40,232},{48,32},{56,248},{... | collective-permute-start | bytes 245768 | tf_op jit(solution)/shard_map/ppermute | solution.py:306
  16.2 0.0 collective-permute-start.4
  16.2 1.6 %segment_spikes.1.before.spikes = f32[5,128,8,128]{3,2,1,0:T(8,128)S(1)} custom-call(f32[2,8,64,128]{3,2,1,0:T(8,128)S(1)} %get-tuple-element.24.l2, f32[2,8,64,128]{3,2,1,0:T(8,128)S(1)} %get-tuple-element.25.l1, f32[2,8,64,128]{3,2,1,0:T(8,128)S(1)} %get-tuple-element.26.u1, f32[2,8,64,128]{3,2,1,0:T(8,128)S(1)} %get-tuple-element.27.u2, ...), custom_call_target="tpu_custom_call" | custom-call | tf_op jit(solution)/shard_map/segment_spikes/pallas_call | solution.py:292
  17.8 0.0 collective-permute-done.6.by2
  17.8 2.1 %collective-permute-done.5.by3 = f32[20,8,128]{2,1,0:T(8,128)S(1)} collective-permute-done((f32[20,8,128]{2,1,0:T(8,128)S(1)}, f32[20,8,128]{2,1,0:T(8,128)S(1)}, u32[]{:S(2)}, u32[]{:S(2)}) %collective-permute-start.5) | collective-permute-done | bytes 81952 | tf_op jit(solution)/shard_map/ppermute | solution.py:306
  19.9 0.0 collective-permute-done.4.by1
  19.9 0.1 y_solve.1
  20.1 0.4 %collective-permute-start.7 = (f32[4,8,128]{2,1,0:T(8,128)S(1)}, f32[4,8,128]{2,1,0:T(8,128)S(1)}, u32[]{:S(2)}, u32[]{:S(2)}) collective-permute-start(f32[4,8,128]{2,1,0:T(8,128)S(1)} %get-tuple-element.29), channel_id=1, source_target_pairs={{0,8},{8,0},{16,24},{24,16},{32,40},{40,32},{48,56},{56,48},{64,72... | collective-permute-start | bytes 49160 | tf_op jit(solution)/shard_map/ppermute | solution.py:306
  20.5 0.9 %combine_odd.1.partial = f32[16,64,128]{2,1,0:T(8,128)} custom-call(f32[4,8,128]{2,1,0:T(8,128)S(1)} %get-tuple-element.30.ends, f32[5,128,8,128]{3,2,1,0:T(8,128)S(1)} %segment_spikes.1.before.spikes), custom_call_target="tpu_custom_call" | custom-call | tf_op jit(solution)/shard_map/combine_odd/pallas_call | solution.py:292
  21.4 0.0 collective-permute-done.7.ends
  21.4 0.1 combine_even.1
  (1 shorter events, 0.0 us)
Async XLA Ops:
  2.4 4.3 %collective-permute-start = (f32[20,8,128]{2,1,0:T(8,128)S(1)}, f32[20,8,128]{2,1,0:T(8,128)S(1)}, u32[]{:S(2)}, u32[]{:S(2)}) collective-permute-start(f32[20,8,128]{2,1,0:T(8,128)S(1)} %get-tuple-element.18.own_ref), channel_id=1, source_target_pairs={{0,8},{8,0},{16,24},{24,16},{32,40},{40,32},{48,56},{56,48},{64,72... | collective-permute-start | bytes 245768 | tf_op jit(solution)/shard_map/ppermute | solution.py:306
  6.7 4.9 %collective-permute-start.3 = (f32[20,8,128]{2,1,0:T(8,128)S(1)}, f32[20,8,128]{2,1,0:T(8,128)S(1)}, u32[]{:S(2)}, u32[]{:S(2)}) collective-permute-start(f32[20,8,128]{2,1,0:T(8,128)S(1)} %get-tuple-element.19.own_ref.after), channel_id=1, source_target_pairs={{0,64},{8,40},{16,80},{24,56},{32,96},{40,8},{48,112},{56,24},{64,... | collective-permute-start | bytes 245768 | tf_op jit(solution)/shard_map/ppermute | solution.py:306
  7.8 4.7 %collective-permute-start.2 = (f32[20,8,128]{2,1,0:T(8,128)S(1)}, f32[20,8,128]{2,1,0:T(8,128)S(1)}, u32[]{:S(2)}, u32[]{:S(2)}) collective-permute-start(f32[20,8,128]{2,1,0:T(8,128)S(1)} %get-tuple-element.19.own_ref.after), channel_id=1, source_target_pairs={{0,64},{8,56},{16,80},{24,40},{32,96},{40,24},{48,112},{56,8},{64,... | collective-permute-start | bytes 245768 | tf_op jit(solution)/shard_map/ppermute | solution.py:306
  8.6 3.8 %collective-permute-start.1 = (f32[20,8,128]{2,1,0:T(8,128)S(1)}, f32[20,8,128]{2,1,0:T(8,128)S(1)}, u32[]{:S(2)}, u32[]{:S(2)}) collective-permute-start(f32[20,8,128]{2,1,0:T(8,128)S(1)} %get-tuple-element.19.own_ref.after), channel_id=1, source_target_pairs={{0,64},{8,24},{16,80},{24,8},{32,96},{40,56},{48,112},{56,40},{64,... | collective-permute-start | bytes 245768 | tf_op jit(solution)/shard_map/ppermute | solution.py:306
  12.6 5.2 %collective-permute-start.6 = (f32[20,8,128]{2,1,0:T(8,128)S(1)}, f32[20,8,128]{2,1,0:T(8,128)S(1)}, u32[]{:S(2)}, u32[]{:S(2)}) collective-permute-start(f32[20,8,128]{2,1,0:T(8,128)S(1)} %get-tuple-element.20.own_ref), channel_id=1, source_target_pairs={{0,16},{8,136},{16,0},{24,152},{32,48},{40,168},{48,32},{56,184},{... | collective-permute-start | bytes 245768 | tf_op jit(solution)/shard_map/ppermute | solution.py:306
  15.4 4.5 %collective-permute-start.5 = (f32[20,8,128]{2,1,0:T(8,128)S(1)}, f32[20,8,128]{2,1,0:T(8,128)S(1)}, u32[]{:S(2)}, u32[]{:S(2)}) collective-permute-start(f32[20,8,128]{2,1,0:T(8,128)S(1)} %get-tuple-element.20.own_ref), channel_id=1, source_target_pairs={{0,16},{8,200},{16,0},{24,216},{32,48},{40,232},{48,32},{56,248},{... | collective-permute-start | bytes 245768 | tf_op jit(solution)/shard_map/ppermute | solution.py:306
  16.2 3.7 %collective-permute-start.4 = (f32[20,8,128]{2,1,0:T(8,128)S(1)}, f32[20,8,128]{2,1,0:T(8,128)S(1)}, u32[]{:S(2)}, u32[]{:S(2)}) collective-permute-start(f32[20,8,128]{2,1,0:T(8,128)S(1)} %get-tuple-element.20.own_ref), channel_id=1, source_target_pairs={{0,16},{8,72},{16,0},{24,88},{32,48},{40,104},{48,32},{56,120},{64... | collective-permute-start | bytes 245768 | tf_op jit(solution)/shard_map/ppermute | solution.py:306
  20.1 1.3 %collective-permute-start.7 = (f32[4,8,128]{2,1,0:T(8,128)S(1)}, f32[4,8,128]{2,1,0:T(8,128)S(1)}, u32[]{:S(2)}, u32[]{:S(2)}) collective-permute-start(f32[4,8,128]{2,1,0:T(8,128)S(1)} %get-tuple-element.29), channel_id=1, source_target_pairs={{0,8},{8,0},{16,24},{24,16},{32,40},{40,32},{48,56},{56,48},{64,72... | collective-permute-start | bytes 49160 | tf_op jit(solution)/shard_map/ppermute | solution.py:306

commit v6 on v5

--- a/solution.py
+++ b/solution.py
@@ -331,7 +331,7 @@
     chip, core_split = call(
         core_kernel, [port_shape] * 2, [port, exchange(port, 1, 1)], name="core_join"
     )
-    x_near, x_end, x_far = (exchange(chip, k, 8) for k in (2, 6, 4))
+    x_near, x_end, x_far = (exchange(chip, *masks) for masks in ((3, 3), (6, 8), (4, 8)))
     (spikes,) = call(
         spikes_kernel,
         [(5, ROWS) + TILE],

time: 21.6 us -> 21.8 us (level)
  waiting for transfers between devices: 6.1 us -> 7.81 us
  starting transfers between devices: 10.1 us -> 8.59 us
    ppermute x8, waiting for transfers between devices: 6.1 us -> 7.81 us  [exchange(): return lax.ppermute(port, 'lon', pairs)]
    ppermute x8, starting transfers between devices: 10.1 us -> 8.59 us  [exchange(): return lax.ppermute(port, 'lon', pairs)]
  transfers between devices with their start and end apart: 8 -> 8, of which waited for: 4 -> 6; matrix products, arithmetic and copies ran while one was open for 0% -> 0% of each run, Pallas kernels for 11% -> 11%
where the time goes in v6:
time: 21.8 us; the launch traced here: 21.6 us
  starting transfers between devices  8.59 us (39%)
  waiting for transfers between devices  7.81 us (36%)
  Pallas kernels  5.19 us (24%)
    ppermute x8, starting transfers between devices, exchange(): return lax.ppermute(port, 'lon', pairs)  8.59 us
    ppermute x8, waiting for transfers between devices, exchange(): return lax.ppermute(port, 'lon', pairs)  7.81 us
    pallas_call x7, Pallas kernels, call(): pl.pallas_call(kernel, out_shape=[jax.ShapeDtypeStruct(shape, jnp.float32...  5.19 us
  transfers between devices with their start and end apart: 8, of which 6 were waited for; matrix products, arithmetic and copies ran while one was open for 0% of the time, Pallas kernels for 11%

profile of v6, /device:TPU:1, one launch (start us, length us, event | category | flops | bytes accessed | tf_op | source)
XLA Modules:
  0.0 21.6 jit_solution(9175333116507699921)
XLA Ops:
  0.0 2.4 %segment_port.1 = (f32[20,8,128]{2,1,0:T(8,128)S(1)}, f32[2,8,64,128]{3,2,1,0:T(8,128)S(1)}, f32[2,8,64,128]{3,2,1,0:T(8,128)S(1)}, f32[2,8,64,128]{3,2,1,0:T(8,...) custom-call(f32[2,8,64,128]{3,2,1,0:T(8,128)} %bitcast.30, f32[2,8,64,128]{3,2,1,0:T(8,128)} %bitcast.31, ...), custom_call_target="tpu_custom_call" | custom-call | tf_op jit(solution)/shard_map/segment_port/pallas_call | solution.py:292
  2.4 3.3 %collective-permute-start = (f32[20,8,128]{2,1,0:T(8,128)S(1)}, f32[20,8,128]{2,1,0:T(8,128)S(1)}, u32[]{:S(2)}, u32[]{:S(2)}) collective-permute-start(f32[20,8,128]{2,1,0:T(8,128)S(1)} %get-tuple-element.18.own_ref), channel_id=1, source_target_pairs={{0,8},{8,0},{16,24},{24,16},{32,40},{40,32},{48,56},{56,48},{64,72... | collective-permute-start | bytes 245768 | tf_op jit(solution)/shard_map/ppermute | solution.py:306
  5.7 0.9 %collective-permute-done.other_ref = f32[20,8,128]{2,1,0:T(8,128)S(1)} collective-permute-done((f32[20,8,128]{2,1,0:T(8,128)S(1)}, f32[20,8,128]{2,1,0:T(8,128)S(1)}, u32[]{:S(2)}, u32[]{:S(2)}) %collective-permute-start) | collective-permute-done | bytes 81952 | tf_op jit(solution)/shard_map/ppermute | solution.py:306
  6.7 1.1 %collective-permute-start.3 = (f32[20,8,128]{2,1,0:T(8,128)S(1)}, f32[20,8,128]{2,1,0:T(8,128)S(1)}, u32[]{:S(2)}, u32[]{:S(2)}) collective-permute-start(f32[20,8,128]{2,1,0:T(8,128)S(1)} %get-tuple-element.19.own_ref.after), channel_id=1, source_target_pairs={{0,64},{8,40},{16,80},{24,56},{32,96},{40,8},{48,112},{56,24},{64,... | collective-permute-start | bytes 245768 | tf_op jit(solution)/shard_map/ppermute | solution.py:306
  7.8 0.9 %collective-permute-start.2 = (f32[20,8,128]{2,1,0:T(8,128)S(1)}, f32[20,8,128]{2,1,0:T(8,128)S(1)}, u32[]{:S(2)}, u32[]{:S(2)}) collective-permute-start(f32[20,8,128]{2,1,0:T(8,128)S(1)} %get-tuple-element.19.own_ref.after), channel_id=1, source_target_pairs={{0,64},{8,56},{16,80},{24,40},{32,96},{40,24},{48,112},{56,8},{64,... | collective-permute-start | bytes 245768 | tf_op jit(solution)/shard_map/ppermute | solution.py:306
  8.6 0.0 collective-permute-start.1
  8.7 2.9 %collective-permute-done.3.by2 = f32[20,8,128]{2,1,0:T(8,128)S(1)} collective-permute-done((f32[20,8,128]{2,1,0:T(8,128)S(1)}, f32[20,8,128]{2,1,0:T(8,128)S(1)}, u32[]{:S(2)}, u32[]{:S(2)}) %collective-permute-start.3) | collective-permute-done | bytes 81952 | tf_op jit(solution)/shard_map/ppermute | solution.py:306
  11.6 0.9 %collective-permute-done.2.by3 = f32[20,8,128]{2,1,0:T(8,128)S(1)} collective-permute-done((f32[20,8,128]{2,1,0:T(8,128)S(1)}, f32[20,8,128]{2,1,0:T(8,128)S(1)}, u32[]{:S(2)}, u32[]{:S(2)}) %collective-permute-start.2) | collective-permute-done | bytes 81952 | tf_op jit(solution)/shard_map/ppermute | solution.py:306
  12.5 0.9 %collective-permute-done.1.by1 = f32[20,8,128]{2,1,0:T(8,128)S(1)} collective-permute-done((f32[20,8,128]{2,1,0:T(8,128)S(1)}, f32[20,8,128]{2,1,0:T(8,128)S(1)}, u32[]{:S(2)}, u32[]{:S(2)}) %collective-permute-start.1) | collective-permute-done | bytes 81952 | tf_op jit(solution)/shard_map/ppermute | solution.py:306
  13.3 0.1 x_join.1
  13.5 2.2 %collective-permute-start.6 = (f32[20,8,128]{2,1,0:T(8,128)S(1)}, f32[20,8,128]{2,1,0:T(8,128)S(1)}, u32[]{:S(2)}, u32[]{:S(2)}) collective-permute-start(f32[20,8,128]{2,1,0:T(8,128)S(1)} %get-tuple-element.20.own_ref), channel_id=1, source_target_pairs={{0,16},{8,136},{16,0},{24,152},{32,48},{40,168},{48,32},{56,184},{... | collective-permute-start | bytes 245768 | tf_op jit(solution)/shard_map/ppermute | solution.py:306
  15.6 0.8 %collective-permute-start.5 = (f32[20,8,128]{2,1,0:T(8,128)S(1)}, f32[20,8,128]{2,1,0:T(8,128)S(1)}, u32[]{:S(2)}, u32[]{:S(2)}) collective-permute-start(f32[20,8,128]{2,1,0:T(8,128)S(1)} %get-tuple-element.20.own_ref), channel_id=1, source_target_pairs={{0,16},{8,200},{16,0},{24,216},{32,48},{40,232},{48,32},{56,248},{... | collective-permute-start | bytes 245768 | tf_op jit(solution)/shard_map/ppermute | solution.py:306
  16.4 0.0 collective-permute-start.4
  16.4 1.6 %segment_spikes.1.before.spikes = f32[5,128,8,128]{3,2,1,0:T(8,128)S(1)} custom-call(f32[2,8,64,128]{3,2,1,0:T(8,128)S(1)} %get-tuple-element.24.l2, f32[2,8,64,128]{3,2,1,0:T(8,128)S(1)} %get-tuple-element.25.l1, f32[2,8,64,128]{3,2,1,0:T(8,128)S(1)} %get-tuple-element.26.u1, f32[2,8,64,128]{3,2,1,0:T(8,128)S(1)} %get-tuple-element.27.u2, ...), custom_call_target="tpu_custom_call" | custom-call | tf_op jit(solution)/shard_map/segment_spikes/pallas_call | solution.py:292
  18.0 0.3 %collective-permute-done.6.by2 = f32[20,8,128]{2,1,0:T(8,128)S(1)} collective-permute-done((f32[20,8,128]{2,1,0:T(8,128)S(1)}, f32[20,8,128]{2,1,0:T(8,128)S(1)}, u32[]{:S(2)}, u32[]{:S(2)}) %collective-permute-start.6) | collective-permute-done | bytes 81952 | tf_op jit(solution)/shard_map/ppermute | solution.py:306
  18.3 1.8 %collective-permute-done.5.by3 = f32[20,8,128]{2,1,0:T(8,128)S(1)} collective-permute-done((f32[20,8,128]{2,1,0:T(8,128)S(1)}, f32[20,8,128]{2,1,0:T(8,128)S(1)}, u32[]{:S(2)}, u32[]{:S(2)}) %collective-permute-start.5) | collective-permute-done | bytes 81952 | tf_op jit(solution)/shard_map/ppermute | solution.py:306
  20.1 0.0 collective-permute-done.4.by1
  20.2 0.1 y_solve.1
  20.3 0.3 %collective-permute-start.7 = (f32[4,8,128]{2,1,0:T(8,128)S(1)}, f32[4,8,128]{2,1,0:T(8,128)S(1)}, u32[]{:S(2)}, u32[]{:S(2)}) collective-permute-start(f32[4,8,128]{2,1,0:T(8,128)S(1)} %get-tuple-element.29), channel_id=1, source_target_pairs={{0,8},{8,0},{16,24},{24,16},{32,40},{40,32},{48,56},{56,48},{64,72... | collective-permute-start | bytes 49160 | tf_op jit(solution)/shard_map/ppermute | solution.py:306
  20.6 0.9 %combine_odd.1.partial = f32[16,64,128]{2,1,0:T(8,128)} custom-call(f32[4,8,128]{2,1,0:T(8,128)S(1)} %get-tuple-element.30.ends, f32[5,128,8,128]{3,2,1,0:T(8,128)S(1)} %segment_spikes.1.before.spikes), custom_call_target="tpu_custom_call" | custom-call | tf_op jit(solution)/shard_map/combine_odd/pallas_call | solution.py:292
  21.5 0.1 collective-permute-done.7.ends
  21.6 0.1 combine_even.1
  (1 shorter events, 0.0 us)
Async XLA Ops:
  2.4 4.3 %collective-permute-start = (f32[20,8,128]{2,1,0:T(8,128)S(1)}, f32[20,8,128]{2,1,0:T(8,128)S(1)}, u32[]{:S(2)}, u32[]{:S(2)}) collective-permute-start(f32[20,8,128]{2,1,0:T(8,128)S(1)} %get-tuple-element.18.own_ref), channel_id=1, source_target_pairs={{0,8},{8,0},{16,24},{24,16},{32,40},{40,32},{48,56},{56,48},{64,72... | collective-permute-start | bytes 245768 | tf_op jit(solution)/shard_map/ppermute | solution.py:306
  6.7 4.9 %collective-permute-start.3 = (f32[20,8,128]{2,1,0:T(8,128)S(1)}, f32[20,8,128]{2,1,0:T(8,128)S(1)}, u32[]{:S(2)}, u32[]{:S(2)}) collective-permute-start(f32[20,8,128]{2,1,0:T(8,128)S(1)} %get-tuple-element.19.own_ref.after), channel_id=1, source_target_pairs={{0,64},{8,40},{16,80},{24,56},{32,96},{40,8},{48,112},{56,24},{64,... | collective-permute-start | bytes 245768 | tf_op jit(solution)/shard_map/ppermute | solution.py:306
  7.8 4.7 %collective-permute-start.2 = (f32[20,8,128]{2,1,0:T(8,128)S(1)}, f32[20,8,128]{2,1,0:T(8,128)S(1)}, u32[]{:S(2)}, u32[]{:S(2)}) collective-permute-start(f32[20,8,128]{2,1,0:T(8,128)S(1)} %get-tuple-element.19.own_ref.after), channel_id=1, source_target_pairs={{0,64},{8,56},{16,80},{24,40},{32,96},{40,24},{48,112},{56,8},{64,... | collective-permute-start | bytes 245768 | tf_op jit(solution)/shard_map/ppermute | solution.py:306
  8.6 4.7 %collective-permute-start.1 = (f32[20,8,128]{2,1,0:T(8,128)S(1)}, f32[20,8,128]{2,1,0:T(8,128)S(1)}, u32[]{:S(2)}, u32[]{:S(2)}) collective-permute-start(f32[20,8,128]{2,1,0:T(8,128)S(1)} %get-tuple-element.19.own_ref.after), channel_id=1, source_target_pairs={{0,24},{8,16},{16,8},{24,0},{32,56},{40,48},{48,40},{56,32},{64,88... | collective-permute-start | bytes 245768 | tf_op jit(solution)/shard_map/ppermute | solution.py:306
  13.5 4.9 %collective-permute-start.6 = (f32[20,8,128]{2,1,0:T(8,128)S(1)}, f32[20,8,128]{2,1,0:T(8,128)S(1)}, u32[]{:S(2)}, u32[]{:S(2)}) collective-permute-start(f32[20,8,128]{2,1,0:T(8,128)S(1)} %get-tuple-element.20.own_ref), channel_id=1, source_target_pairs={{0,16},{8,136},{16,0},{24,152},{32,48},{40,168},{48,32},{56,184},{... | collective-permute-start | bytes 245768 | tf_op jit(solution)/shard_map/ppermute | solution.py:306
  15.6 4.5 %collective-permute-start.5 = (f32[20,8,128]{2,1,0:T(8,128)S(1)}, f32[20,8,128]{2,1,0:T(8,128)S(1)}, u32[]{:S(2)}, u32[]{:S(2)}) collective-permute-start(f32[20,8,128]{2,1,0:T(8,128)S(1)} %get-tuple-element.20.own_ref), channel_id=1, source_target_pairs={{0,16},{8,200},{16,0},{24,216},{32,48},{40,232},{48,32},{56,248},{... | collective-permute-start | bytes 245768 | tf_op jit(solution)/shard_map/ppermute | solution.py:306
  16.4 3.7 %collective-permute-start.4 = (f32[20,8,128]{2,1,0:T(8,128)S(1)}, f32[20,8,128]{2,1,0:T(8,128)S(1)}, u32[]{:S(2)}, u32[]{:S(2)}) collective-permute-start(f32[20,8,128]{2,1,0:T(8,128)S(1)} %get-tuple-element.20.own_ref), channel_id=1, source_target_pairs={{0,16},{8,72},{16,0},{24,88},{32,48},{40,104},{48,32},{56,120},{64... | collective-permute-start | bytes 245768 | tf_op jit(solution)/shard_map/ppermute | solution.py:306
  20.3 1.3 %collective-permute-start.7 = (f32[4,8,128]{2,1,0:T(8,128)S(1)}, f32[4,8,128]{2,1,0:T(8,128)S(1)}, u32[]{:S(2)}, u32[]{:S(2)}) collective-permute-start(f32[4,8,128]{2,1,0:T(8,128)S(1)} %get-tuple-element.29), channel_id=1, source_target_pairs={{0,8},{8,0},{16,24},{24,16},{32,40},{40,32},{48,56},{56,48},{64,72... | collective-permute-start | bytes 49160 | tf_op jit(solution)/shard_map/ppermute | solution.py:306

commit v7 on v5

--- a/solution.py
+++ b/solution.py
@@ -209,7 +209,7 @@
     return place % 2 == 1, place // 2 == 1
 
 
-def group_kernel(own_ref, by1, by3, by2, out, split_pair, split_top):
+def group_kernel(own_ref, by1, by3, by2, before, out, split_pair, split_top):
     low_bit, high_bit = bits(2)
     first, second = swap_if(low_bit, read_port(own_ref), read_port(by1))
     split = split_of(first, second)
@@ -231,7 +231,7 @@
     return new_w, new_e
 
 
-def solve_kernel(own_ref, by1, by3, by2, top_x, pair_x, core, before, low_out, high_out):
+def solve_kernel(own_ref, by1, by3, by2, top_x, pair_x, core, low_out, high_out):
     low_bit, high_bit = bits(8)
     first, second = swap_if(low_bit, read_port(own_ref), read_port(by1))
     split_mine = split_of(first, second)
@@ -339,12 +339,12 @@
         scratch=[pltpu.VMEM((ROWS,) + TILE, jnp.float32)] * 2,
         name="segment_spikes",
     )
-    group, pair_x, top_x = call(group_kernel, [port_shape] * 3, [chip, x_near, x_end, x_far], name="x_join")
+    group, pair_x, top_x = call(group_kernel, [port_shape] * 3, [chip, x_near, x_end, x_far, spikes], name="x_join")
     y_near, y_end, y_far = (exchange(group, k, 2) for k in (8, 24, 16))
     low_ends, high_ends = call(
         solve_kernel,
         [(4,) + TILE] * 2,
-        [group, y_near, y_end, y_far, top_x, pair_x, core_split, spikes],
+        [group, y_near, y_end, y_far, top_x, pair_x, core_split],
         name="y_solve",
     )
     received = exchange(low_ends, 1, 1)

time: 21.6 us -> 21.6 us (level)
  transfers between devices with their start and end apart: 8 -> 8, of which waited for: 4 -> 5; matrix products, arithmetic and copies ran while one was open for 0% -> 0% of each run, Pallas kernels for 11% -> 11%
where the time goes in v7:
time: 21.6 us; the launch traced here: 21.5 us
  starting transfers between devices  10.1 us (47%)
  waiting for transfers between devices  6.11 us (28%)
  Pallas kernels  5.22 us (24%)
    ppermute x8, starting transfers between devices, exchange(): return lax.ppermute(port, 'lon', pairs)  10.1 us
    ppermute x8, waiting for transfers between devices, exchange(): return lax.ppermute(port, 'lon', pairs)  6.11 us
    pallas_call x7, Pallas kernels, call(): pl.pallas_call(kernel, out_shape=[jax.ShapeDtypeStruct(shape, jnp.float32...  5.22 us
  transfers between devices with their start and end apart: 8, of which 5 were waited for; matrix products, arithmetic and copies ran while one was open for 0% of the time, Pallas kernels for 11%

profile of v7, /device:TPU:1, one launch (start us, length us, event | category | flops | bytes accessed | tf_op | source)
XLA Modules:
  0.0 21.5 jit_solution(7912750711751875795)
XLA Ops:
  0.0 2.4 %segment_port.1 = (f32[20,8,128]{2,1,0:T(8,128)S(1)}, f32[2,8,64,128]{3,2,1,0:T(8,128)S(1)}, f32[2,8,64,128]{3,2,1,0:T(8,128)S(1)}, f32[2,8,64,128]{3,2,1,0:T(8,...) custom-call(f32[2,8,64,128]{3,2,1,0:T(8,128)} %bitcast.30, f32[2,8,64,128]{3,2,1,0:T(8,128)} %bitcast.31, ...), custom_call_target="tpu_custom_call" | custom-call | tf_op jit(solution)/shard_map/segment_port/pallas_call | solution.py:292
  2.4 3.3 %collective-permute-start = (f32[20,8,128]{2,1,0:T(8,128)S(1)}, f32[20,8,128]{2,1,0:T(8,128)S(1)}, u32[]{:S(2)}, u32[]{:S(2)}) collective-permute-start(f32[20,8,128]{2,1,0:T(8,128)S(1)} %get-tuple-element.18.own_ref), channel_id=1, source_target_pairs={{0,8},{8,0},{16,24},{24,16},{32,40},{40,32},{48,56},{56,48},{64,72... | collective-permute-start | bytes 245768 | tf_op jit(solution)/shard_map/ppermute | solution.py:306
  5.7 0.9 %collective-permute-done.other_ref = f32[20,8,128]{2,1,0:T(8,128)S(1)} collective-permute-done((f32[20,8,128]{2,1,0:T(8,128)S(1)}, f32[20,8,128]{2,1,0:T(8,128)S(1)}, u32[]{:S(2)}, u32[]{:S(2)}) %collective-permute-start) | collective-permute-done | bytes 81952 | tf_op jit(solution)/shard_map/ppermute | solution.py:306
  6.7 1.1 %collective-permute-start.3 = (f32[20,8,128]{2,1,0:T(8,128)S(1)}, f32[20,8,128]{2,1,0:T(8,128)S(1)}, u32[]{:S(2)}, u32[]{:S(2)}) collective-permute-start(f32[20,8,128]{2,1,0:T(8,128)S(1)} %get-tuple-element.19.after.own_ref), channel_id=1, source_target_pairs={{0,64},{8,40},{16,80},{24,56},{32,96},{40,8},{48,112},{56,24},{64,... | collective-permute-start | bytes 245768 | tf_op jit(solution)/shard_map/ppermute | solution.py:306
  7.8 0.9 %collective-permute-start.2 = (f32[20,8,128]{2,1,0:T(8,128)S(1)}, f32[20,8,128]{2,1,0:T(8,128)S(1)}, u32[]{:S(2)}, u32[]{:S(2)}) collective-permute-start(f32[20,8,128]{2,1,0:T(8,128)S(1)} %get-tuple-element.19.after.own_ref), channel_id=1, source_target_pairs={{0,64},{8,56},{16,80},{24,40},{32,96},{40,24},{48,112},{56,8},{64,... | collective-permute-start | bytes 245768 | tf_op jit(solution)/shard_map/ppermute | solution.py:306
  8.6 0.8 %collective-permute-start.1 = (f32[20,8,128]{2,1,0:T(8,128)S(1)}, f32[20,8,128]{2,1,0:T(8,128)S(1)}, u32[]{:S(2)}, u32[]{:S(2)}) collective-permute-start(f32[20,8,128]{2,1,0:T(8,128)S(1)} %get-tuple-element.19.after.own_ref), channel_id=1, source_target_pairs={{0,64},{8,24},{16,80},{24,8},{32,96},{40,56},{48,112},{56,40},{64,... | collective-permute-start | bytes 245768 | tf_op jit(solution)/shard_map/ppermute | solution.py:306
  9.4 1.6 %segment_spikes.1.before.spikes = f32[5,128,8,128]{3,2,1,0:T(8,128)S(1)} custom-call(f32[2,8,64,128]{3,2,1,0:T(8,128)S(1)} %get-tuple-element.20.l2, f32[2,8,64,128]{3,2,1,0:T(8,128)S(1)} %get-tuple-element.21.l1, f32[2,8,64,128]{3,2,1,0:T(8,128)S(1)} %get-tuple-element.22.u1, f32[2,8,64,128]{3,2,1,0:T(8,128)S(1)} %get-tuple-element.23.u2, ...), custom_call_target="tpu_custom_call" | custom-call | tf_op jit(solution)/shard_map/segment_spikes/pallas_call | solution.py:292
  11.0 0.6 %collective-permute-done.3.by2 = f32[20,8,128]{2,1,0:T(8,128)S(1)} collective-permute-done((f32[20,8,128]{2,1,0:T(8,128)S(1)}, f32[20,8,128]{2,1,0:T(8,128)S(1)}, u32[]{:S(2)}, u32[]{:S(2)}) %collective-permute-start.3) | collective-permute-done | bytes 81952 | tf_op jit(solution)/shard_map/ppermute | solution.py:306
  11.6 0.9 %collective-permute-done.2.by3 = f32[20,8,128]{2,1,0:T(8,128)S(1)} collective-permute-done((f32[20,8,128]{2,1,0:T(8,128)S(1)}, f32[20,8,128]{2,1,0:T(8,128)S(1)}, u32[]{:S(2)}, u32[]{:S(2)}) %collective-permute-start.2) | collective-permute-done | bytes 81952 | tf_op jit(solution)/shard_map/ppermute | solution.py:306
  12.5 0.0 collective-permute-done.1.by1
  12.5 0.1 x_join.1
  12.6 2.8 %collective-permute-start.6 = (f32[20,8,128]{2,1,0:T(8,128)S(1)}, f32[20,8,128]{2,1,0:T(8,128)S(1)}, u32[]{:S(2)}, u32[]{:S(2)}) collective-permute-start(f32[20,8,128]{2,1,0:T(8,128)S(1)} %get-tuple-element.25.own_ref), channel_id=1, source_target_pairs={{0,16},{8,136},{16,0},{24,152},{32,48},{40,168},{48,32},{56,184},{... | collective-permute-start | bytes 245768 | tf_op jit(solution)/shard_map/ppermute | solution.py:306
  15.4 0.8 %collective-permute-start.5 = (f32[20,8,128]{2,1,0:T(8,128)S(1)}, f32[20,8,128]{2,1,0:T(8,128)S(1)}, u32[]{:S(2)}, u32[]{:S(2)}) collective-permute-start(f32[20,8,128]{2,1,0:T(8,128)S(1)} %get-tuple-element.25.own_ref), channel_id=1, source_target_pairs={{0,16},{8,200},{16,0},{24,216},{32,48},{40,232},{48,32},{56,248},{... | collective-permute-start | bytes 245768 | tf_op jit(solution)/shard_map/ppermute | solution.py:306
  16.2 0.0 collective-permute-start.4
  16.2 1.3 %collective-permute-done.6.by2 = f32[20,8,128]{2,1,0:T(8,128)S(1)} collective-permute-done((f32[20,8,128]{2,1,0:T(8,128)S(1)}, f32[20,8,128]{2,1,0:T(8,128)S(1)}, u32[]{:S(2)}, u32[]{:S(2)}) %collective-permute-start.6) | collective-permute-done | bytes 81952 | tf_op jit(solution)/shard_map/ppermute | solution.py:306
  17.5 2.5 %collective-permute-done.5.by3 = f32[20,8,128]{2,1,0:T(8,128)S(1)} collective-permute-done((f32[20,8,128]{2,1,0:T(8,128)S(1)}, f32[20,8,128]{2,1,0:T(8,128)S(1)}, u32[]{:S(2)}, u32[]{:S(2)}) %collective-permute-start.5) | collective-permute-done | bytes 81952 | tf_op jit(solution)/shard_map/ppermute | solution.py:306
  19.9 0.0 collective-permute-done.4.by1
  19.9 0.1 y_solve.1
  20.1 0.4 %collective-permute-start.7 = (f32[4,8,128]{2,1,0:T(8,128)S(1)}, f32[4,8,128]{2,1,0:T(8,128)S(1)}, u32[]{:S(2)}, u32[]{:S(2)}) collective-permute-start(f32[4,8,128]{2,1,0:T(8,128)S(1)} %get-tuple-element.29), channel_id=1, source_target_pairs={{0,8},{8,0},{16,24},{24,16},{32,40},{40,32},{48,56},{56,48},{64,72... | collective-permute-start | bytes 49160 | tf_op jit(solution)/shard_map/ppermute | solution.py:306
  20.5 0.9 %combine_odd.1.partial = f32[16,64,128]{2,1,0:T(8,128)} custom-call(f32[4,8,128]{2,1,0:T(8,128)S(1)} %get-tuple-element.30.ends, f32[5,128,8,128]{3,2,1,0:T(8,128)S(1)} %segment_spikes.1.before.spikes), custom_call_target="tpu_custom_call" | custom-call | tf_op jit(solution)/shard_map/combine_odd/pallas_call | solution.py:292
  21.4 0.0 collective-permute-done.7.ends
  21.4 0.1 combine_even.1
  (1 shorter events, 0.0 us)
Async XLA Ops:
  2.4 4.3 %collective-permute-start = (f32[20,8,128]{2,1,0:T(8,128)S(1)}, f32[20,8,128]{2,1,0:T(8,128)S(1)}, u32[]{:S(2)}, u32[]{:S(2)}) collective-permute-start(f32[20,8,128]{2,1,0:T(8,128)S(1)} %get-tuple-element.18.own_ref), channel_id=1, source_target_pairs={{0,8},{8,0},{16,24},{24,16},{32,40},{40,32},{48,56},{56,48},{64,72... | collective-permute-start | bytes 245768 | tf_op jit(solution)/shard_map/ppermute | solution.py:306
  6.7 4.9 %collective-permute-start.3 = (f32[20,8,128]{2,1,0:T(8,128)S(1)}, f32[20,8,128]{2,1,0:T(8,128)S(1)}, u32[]{:S(2)}, u32[]{:S(2)}) collective-permute-start(f32[20,8,128]{2,1,0:T(8,128)S(1)} %get-tuple-element.19.after.own_ref), channel_id=1, source_target_pairs={{0,64},{8,40},{16,80},{24,56},{32,96},{40,8},{48,112},{56,24},{64,... | collective-permute-start | bytes 245768 | tf_op jit(solution)/shard_map/ppermute | solution.py:306
  7.8 4.7 %collective-permute-start.2 = (f32[20,8,128]{2,1,0:T(8,128)S(1)}, f32[20,8,128]{2,1,0:T(8,128)S(1)}, u32[]{:S(2)}, u32[]{:S(2)}) collective-permute-start(f32[20,8,128]{2,1,0:T(8,128)S(1)} %get-tuple-element.19.after.own_ref), channel_id=1, source_target_pairs={{0,64},{8,56},{16,80},{24,40},{32,96},{40,24},{48,112},{56,8},{64,... | collective-permute-start | bytes 245768 | tf_op jit(solution)/shard_map/ppermute | solution.py:306
  8.6 3.8 %collective-permute-start.1 = (f32[20,8,128]{2,1,0:T(8,128)S(1)}, f32[20,8,128]{2,1,0:T(8,128)S(1)}, u32[]{:S(2)}, u32[]{:S(2)}) collective-permute-start(f32[20,8,128]{2,1,0:T(8,128)S(1)} %get-tuple-element.19.after.own_ref), channel_id=1, source_target_pairs={{0,64},{8,24},{16,80},{24,8},{32,96},{40,56},{48,112},{56,40},{64,... | collective-permute-start | bytes 245768 | tf_op jit(solution)/shard_map/ppermute | solution.py:306
  12.6 4.9 %collective-permute-start.6 = (f32[20,8,128]{2,1,0:T(8,128)S(1)}, f32[20,8,128]{2,1,0:T(8,128)S(1)}, u32[]{:S(2)}, u32[]{:S(2)}) collective-permute-start(f32[20,8,128]{2,1,0:T(8,128)S(1)} %get-tuple-element.25.own_ref), channel_id=1, source_target_pairs={{0,16},{8,136},{16,0},{24,152},{32,48},{40,168},{48,32},{56,184},{... | collective-permute-start | bytes 245768 | tf_op jit(solution)/shard_map/ppermute | solution.py:306
  15.4 4.5 %collective-permute-start.5 = (f32[20,8,128]{2,1,0:T(8,128)S(1)}, f32[20,8,128]{2,1,0:T(8,128)S(1)}, u32[]{:S(2)}, u32[]{:S(2)}) collective-permute-start(f32[20,8,128]{2,1,0:T(8,128)S(1)} %get-tuple-element.25.own_ref), channel_id=1, source_target_pairs={{0,16},{8,200},{16,0},{24,216},{32,48},{40,232},{48,32},{56,248},{... | collective-permute-start | bytes 245768 | tf_op jit(solution)/shard_map/ppermute | solution.py:306
  16.2 3.7 %collective-permute-start.4 = (f32[20,8,128]{2,1,0:T(8,128)S(1)}, f32[20,8,128]{2,1,0:T(8,128)S(1)}, u32[]{:S(2)}, u32[]{:S(2)}) collective-permute-start(f32[20,8,128]{2,1,0:T(8,128)S(1)} %get-tuple-element.25.own_ref), channel_id=1, source_target_pairs={{0,16},{8,72},{16,0},{24,88},{32,48},{40,104},{48,32},{56,120},{64... | collective-permute-start | bytes 245768 | tf_op jit(solution)/shard_map/ppermute | solution.py:306
  20.1 1.3 %collective-permute-start.7 = (f32[4,8,128]{2,1,0:T(8,128)S(1)}, f32[4,8,128]{2,1,0:T(8,128)S(1)}, u32[]{:S(2)}, u32[]{:S(2)}) collective-permute-start(f32[4,8,128]{2,1,0:T(8,128)S(1)} %get-tuple-element.29), channel_id=1, source_target_pairs={{0,8},{8,0},{16,24},{24,16},{32,40},{40,32},{48,56},{56,48},{64,72... | collective-permute-start | bytes 49160 | tf_op jit(solution)/shard_map/ppermute | solution.py:306
